TPU v7x, 128 devices: a whole 4x4x4 slice. The times are simulated.
128 devices in a mesh: pair: 32 (over x, y, core), slab: 4 (over z).
Axes of the slice: x: 4, y: 4, z: 4, core: 2. Of those that a mesh axis runs over, the one named last changes fastest.
Arguments:
- amplitudes: bfloat16 [32, 32, 160000], P('pair'), may hold values from -6 to 6
- integrals: bfloat16 [160000, 1024], P('pair', 'slab'), may hold values from -0.0390625 to 0.0390625
- virt_irrep: int32 [400], replicated, may hold values from 0 to 7
- occ_energy: float32 [32], replicated, may hold values from -1.2 to -0.3
- slab_energy: float32 [32], replicated, may hold values from 0.1 to 1.5
Outputs:
- update: float32 [32, 32, 32, 32], P('pair', None, 'slab')
All inputs are finite; a program needn't handle non-finite values.
Results may differ from a plain program's by a relative error of at most 0.0003.
Values may be sent and summed in bfloat16 or wider, within the bound.
A program may use at most 256 MiB of HBM per device.

v0:
```python
import jax
import jax.numpy as jnp
from jax import lax
from jax.sharding import PartitionSpec as P


def local(amplitudes, integrals, virt_irrep, occ_energy, slab_energy):
    slab_count = lax.axis_size("slab")
    pair_index = lax.axis_index("pair")
    slab_index = lax.axis_index("slab")
    occ_local, occupied, virt_pairs = amplitudes.shape
    rows_local, cols_local = integrals.shape
    slab_virt = slab_energy.shape[0]
    first_local = slab_virt // slab_count
    irrep_cd = jnp.bitwise_xor(virt_irrep[:, None], virt_irrep[None, :]).reshape(-1)
    rows_irrep = lax.dynamic_slice_in_dim(irrep_cd, pair_index * rows_local, rows_local, 0)
    slab_irrep = virt_irrep[:slab_virt]
    irrep_ab = jnp.bitwise_xor(slab_irrep[:, None], slab_irrep[None, :]).reshape(-1)
    cols_irrep = lax.dynamic_slice_in_dim(irrep_ab, slab_index * cols_local, cols_local, 0)
    masked = jnp.where(
        rows_irrep[:, None] == cols_irrep[None, :], integrals, jnp.zeros((), integrals.dtype)
    )
    gathered = lax.all_to_all(amplitudes, "pair", split_axis=2, concat_axis=0, tiled=True)
    count = occ_local * lax.axis_size("pair")
    flat_rows = gathered.reshape(count * occupied, rows_local)
    product = jnp.dot(flat_rows, masked, preferred_element_type=jnp.float32)
    summed = lax.psum_scatter(
        product.reshape(count, occupied, cols_local), "pair", scatter_dimension=0, tiled=True
    )
    residual = summed.reshape(occ_local, occupied, first_local, slab_virt)
    swapped = lax.all_to_all(
        lax.all_to_all(residual, "pair", split_axis=1, concat_axis=0, tiled=True),
        "slab",
        split_axis=3,
        concat_axis=2,
        tiled=True,
    )
    mirrored = jnp.transpose(swapped, (1, 0, 3, 2))
    symmetric = residual + mirrored
    energy_i = lax.dynamic_slice_in_dim(occ_energy, pair_index * occ_local, occ_local, 0)
    energy_a = lax.dynamic_slice_in_dim(slab_energy, slab_index * first_local, first_local, 0)
    denominator = (
        energy_a[None, None, :, None]
        + slab_energy[None, None, None, :]
        - energy_i[:, None, None, None]
        - occ_energy[None, :, None, None]
    )
    return symmetric / denominator


def solution(mesh):
    placed = (P("pair", None, None), P("pair", "slab"), P(), P(), P())
    return jax.shard_map(
        local, mesh=mesh, in_specs=placed, out_specs=P("pair", None, "slab", None), check_vma=False
    )
```

profile of v0, /device:TPU:0, one launch (start us, length us, event | category | flops | bytes accessed | tf_op | source)
XLA Modules:
  0.0 1595.9 jit_solution(8532723662407201712)
XLA Ops:
  6.5 145.4 %copy.33 = bf16[1,32,160000]{1,0,2:T(2,128)(2,1)} copy(bf16[1,32,160000]{2,1,0:T(8,128)(2,1)} %param.5) | data formatting | bytes 20480000 | tf_op args[0]
  152.0 0.5 broadcast.58
  152.5 870.8 %reduce = bf16[160000,32]{1,0:T(8,128)(2,1)} reduce(bf16[160000,1,32]{2,1,0:T(2,128)(2,1)} %bitcast.15, bf16[]{:T(256)} %broadcast.58), dimensions={1}, to_apply=%bitcast.15.reduce_sub_computation | reduce | bytes 20480002
  1023.3 46.9 %reshape.76 = bf16[32,2,80000]{2,1,0:T(2,128)(2,1)} reshape(bf16[160000,32]{1,0:T(8,128)(2,1)} %reduce) | data formatting | bytes 20480000
  1070.2 0.0 slice-start
  1070.2 0.0 copy-start
  1070.2 7.7 all-to-all-start
  1077.8 0.2 reduce-scatter.2.cloned.1.call-start
  1078.1 0.0 slice-done
  1078.1 0.1 broadcast_xor_fusion.1
  1078.2 0.1 xor.41
  1078.2 0.0 copy-done
  1078.2 0.1 broadcast_xor_fusion
  1078.4 0.7 xor.37
  1079.1 0.1 dynamic_slice.13
  1079.2 0.1 dynamic_slice.12
  1079.2 140.0 %all-to-all-done = bf16[32,2,80000]{2,1,0:T(2,128)(2,1)} async-done(((bf16[32,2,80000]{2,1,0:T(2,128)(2,1)}), bf16[32,2,80000]{2,1,0:T(2,128)(2,1)}, u32[]{:S(2)}, u32[]{:S(2)}) %all-to-all-start) | async-done | bytes 10240032 | tf_op jit(solution)/shard_map/all_to_all | solution.py:23
  1219.2 51.4 %reshape.77 = bf16[160000,1,32]{2,1,0:T(2,128)(2,1)} reshape(bf16[32,2,80000]{2,1,0:T(2,128)(2,1)} %all-to-all-done) | data formatting | bytes 20480000
  1270.6 147.3 %copy.34 = bf16[1,32,160000]{2,1,0:T(8,128)(2,1)} copy(bf16[1,32,160000]{1,0,2:T(2,128)(2,1)} %bitcast.16) | data formatting | bytes 20480000 | tf_op jit(solution)/shard_map/all_to_all | solution.py:23
  1417.9 21.7 %all_to_all.34 = bf16[1,32,32,5000]{3,2,1,0:T(8,128)(2,1)} reshape(bf16[1,32,160000]{2,1,0:T(8,128)(2,1)} %copy.34) | data formatting | bytes 20480000 | tf_op jit(solution)/shard_map/all_to_all | solution.py:23
  1439.6 13.5 copy.35
  1453.1 0.0 copy-start.1
  1453.1 0.0 copy-start.2
  1453.2 8.5 fusion.3
  1461.6 1.3 copy.36
  1462.9 0.0 reduce-scatter.2.cloned.1.call-update
  1463.0 97.9 %reduce-scatter.2.cloned.1.call-done = f32[1,32,256]{2,1,0:T(8,128)} async-done(((f32[32,32,256]{2,1,0:T(8,128)}), f32[1,32,256]{2,1,0:T(8,128)}) %reduce-scatter.2.cloned.1.call-update) | async-done | bytes 32784 | tf_op jit(solution)/shard_map/reduce_scatter | solution.py:27
  1560.9 0.8 reshape.75
  1561.8 0.7 reshape.78
  1562.5 5.2 all-to-all-start.1
  1567.7 0.0 copy-done.1
  1567.7 0.6 dynamic_slice.15
  1568.3 0.0 copy-done.2
  1568.3 0.1 dynamic_slice.14
  1568.4 6.7 all-to-all-done.1
  1575.1 0.6 broadcast.59
  1575.7 0.7 reduce.1
  1576.4 0.1 reshape.79
  1576.5 0.1 copy.38
  1576.7 0.7 reshape.80
  1577.4 4.4 all-to-all-start.2
  1581.8 0.7 add_subtract_fusion
  1582.5 0.1 copy.42
  1582.6 0.1 copy.41
  1582.7 4.6 all-to-all-done.2
  1587.3 0.7 reduce.2
  1588.0 0.1 reshape.81
  1588.1 0.1 subtract_divide_fusion
  1588.3 0.8 copy.43
  (4 shorter events, 0.1 us)
Async XLA Ops:
  1070.2 7.9 slice-start
  1070.2 8.1 copy-start
  1070.2 149.0 %all-to-all-start = ((bf16[32,2,80000]{2,1,0:T(2,128)(2,1)}), bf16[32,2,80000]{2,1,0:T(2,128)(2,1)}, u32[]{:S(2)}, u32[]{:S(2)}) async-start(bf16[32,2,80000]{2,1,0:T(2,128)(2,1)} %reshape.76), calls=%async_computation | async-start | bytes 20480000 | tf_op jit(solution)/shard_map/all_to_all | solution.py:23
  1077.8 483.0 %reduce-scatter.2.cloned.1.call-start = ((), (), s32[]{:S(2)}) async-start(), calls=%async_computation.4 | async-start | bytes 1081344 | tf_op jit(solution)/shard_map/reduce_scatter | solution.py:27
  1453.1 114.6 %copy-start.1 = (f32[32]{0:T(128)S(1)}, f32[32]{0:T(128)}, u32[]{:S(2)}) copy-start(f32[32]{0:T(128)} %param.8) | copy-start | bytes 388
  1453.1 115.2 %copy-start.2 = (f32[32]{0:T(128)S(1)}, f32[32]{0:T(128)}, u32[]{:S(2)}) copy-start(f32[32]{0:T(128)} %param.9) | copy-start | bytes 388
  1562.5 12.7 all-to-all-start.1
  1577.4 9.9 all-to-all-start.2
Sparse Core Ops, SparseCore 0:
  1463.1 97.7 reduce-scatter.1
where the time goes:
time: 1620 us; the launch traced here: 1600 us
  other arithmetic  873 us (54%)
  local copies, waits for them, and re-layouts  434 us (27%)
  waiting for transfers between devices  249 us (15%)
  starting transfers between devices  17.5 us (1%)
    unnamed x1, other arithmetic  871 us
    unnamed x15, local copies, waits for them, and re-layouts  246 us
    all_to_all x3, local copies, waits for them, and re-layouts, local(): lax.all_to_all(amplitudes, 'pair', split_axis=2, concat_axis=0, tiled=True)  183 us
    all_to_all x1, waiting for transfers between devices, local(): lax.all_to_all(amplitudes, 'pair', split_axis=2, concat_axis=0, tiled=True)  140 us
    reduce_scatter x1, waiting for transfers between devices, local(): lax.psum_scatter(product.reshape(count, occupied, cols_local), 'pair', sc...  97.9 us
  transfers between devices with their start and end apart: 4, of which 4 were waited for; matrix products, arithmetic and copies ran while one was open for 0% of the time, Pallas kernels for 0%

commit v1 on v0

v1 whole, which is shorter than its diff:
```python
import jax
import jax.numpy as jnp
from jax import lax
from jax.experimental import pallas as pl
from jax.experimental.pallas import tpu as pltpu
from jax.sharding import PartitionSpec as P

F32, BF16, I32 = jnp.float32, jnp.bfloat16, jnp.int32
V, VS, OCC = 400, 32, 32
NZ = 4
ROWS = 5000
GROUPS = ROWS // 8
LANES = 1280
CHUNKS = ((0, 512), (512, 512), (1024, 256))
MARGIN = 16
PARTS = (
    (0, 24, 0, 128, ("z", "x", "y")),
    (0, 24, 128, 128, ("x", "y", "z")),
    (24, 8, 0, 256, ("y", "z", "x")),
)
STEP_DIMS = ((4, 4), (4,), ())


def shift(i, d, n):
    return lax.rem(i + d, n)


def remote(src, dst, send, recv, pair, slab):
    return pltpu.make_async_remote_copy(
        src_ref=src, dst_ref=dst, send_sem=send, recv_sem=recv,
        device_id={"pair": pair, "slab": slab}, device_id_type=pl.DeviceIdType.MESH,
    )


def settle(ref, sem):
    pltpu.make_async_copy(ref, ref, sem).wait()


def kernel(amps, ints, irrep, out, *refs):
    nk = len(CHUNKS)
    abuf, bbuf = refs[:nk], refs[nk:2 * nk]
    bm, bp, perm, vrow, rowirr, colirr, c_ref, d_ref, r_ref = refs[2 * nk:2 * nk + 9]
    q = refs[2 * nk + 9:2 * nk + 18]
    a_send, b_send, a_recv, b_recv, own_sem, m_send, m_recv, q_send, q_recv = refs[2 * nk + 18:]

    p = lax.axis_index("pair")
    s = lax.axis_index("slab")
    x, y, c = p // 8, lax.rem(p // 2, 4), lax.rem(p, 2)

    def pair_at(dx, dy, dc):
        return shift(x, dx, 4) * 8 + shift(y, dy, 4) * 2 + shift(c, dc, 2)

    barrier = pltpu.get_barrier_semaphore()

    def greet(m, carry):
        pl.semaphore_signal(
            barrier, inc=1, device_id={"pair": shift(p, m, 32), "slab": s},
            device_id_type=pl.DeviceIdType.MESH,
        )
        return carry

    lax.fori_loop(1, 32, greet, 0)
    for dz in (1, 2, 3):
        pl.semaphore_signal(
            barrier, inc=1, device_id={"pair": p, "slab": shift(s, dz, NZ)},
            device_id_type=pl.DeviceIdType.MESH,
        )
    pl.semaphore_wait(barrier, 34)

    first_tile = ROWS * p // 128
    lead = lax.rem(p, 16)

    def columns(pair, k):
        tile = ROWS * pair // 128 + 10 * s
        return pl.ds(pl.multiple_of(tile * 128 + CHUNKS[k][0], 128), CHUNKS[k][1])

    def rows_for(slab, k):
        size = CHUNKS[k][1] // 8
        want = 160 * slab - lead + CHUNKS[k][0] // 8
        have = jnp.clip(want, 0, GROUPS - size)
        return pl.ds(have, size), pl.ds(MARGIN + have - want, size)

    def send_amps(k, dx, dy, dc):
        peer = pair_at(dx, dy, dc)
        remote(
            amps.at[:, columns(peer, k)], abuf[k].at[p], a_send, a_recv.at[k], peer, s
        ).start()

    own = []
    for k in range(nk):
        for dz in (1, 3, 2):
            slab = shift(s, dz, NZ)
            source, target = rows_for(slab, k)
            remote(
                ints.at[source], bbuf[k].at[s, target], b_send, b_recv.at[k], p, slab
            ).start()
        source, target = rows_for(s, k)
        own.append(pltpu.make_async_copy(ints.at[source], bbuf[k].at[s, target], own_sem.at[k, 0]))
        own.append(pltpu.make_async_copy(amps.at[:, columns(p, k)], abuf[k].at[p], own_sem.at[k, 1]))
        own[-2].start()
        own[-1].start()
        for dx in (1, 3, 2):
            send_amps(k, dx, dx, 0)

        def send_some(i, carry):
            for dx in (1, 3, 2, 0):
                send_amps(k, dx, i // 2 + dx, lax.rem(i, 2))
            return carry

        lax.fori_loop(1, 8, send_some, 0)

    def fill_perm(t, carry):
        row = lax.broadcasted_iota(I32, (128, 1024), 0) + t * 128
        col = lax.broadcasted_iota(I32, (128, 1024), 1)
        swapped = ((row & 31) << 5) | (row >> 5)
        perm[pl.ds(pl.multiple_of(t * 128, 128), 128), :] = jnp.where(
            swapped == col, F32(1), F32(0)
        ).astype(BF16)
        return carry

    lax.fori_loop(0, 8, fill_perm, 0)
    vrow[...] = jnp.zeros_like(vrow)
    vrow[0:1, 0:V] = irrep[...].astype(F32)
    table = jnp.broadcast_to(vrow[0:1, :], (128, 512)).astype(BF16)
    orb = lax.broadcasted_iota(I32, (128, 1024), 0)
    col = lax.broadcasted_iota(I32, (128, 1024), 1)

    def look_up(lhs, rhs, dims):
        return lax.dot_general(
            lhs, rhs, (dims, ((), ())), preferred_element_type=F32
        ).astype(I32)

    small = table[0:16, 0:128]
    of_a = look_up(small, jnp.where(orb == (col >> 5), F32(1), F32(0)).astype(BF16), ((1,), (0,)))
    of_b = look_up(small, jnp.where(orb == (col & 31), F32(1), F32(0)).astype(BF16), ((1,), (0,)))
    colirr[...] = (of_a ^ of_b)[0:8]

    start = (first_tile + 10 * s) * 128

    def fill_rows(t, carry):
        base = start + t * 256
        c0 = base // V
        row = lax.broadcasted_iota(I32, (256, 512), 0) + base
        orb = lax.broadcasted_iota(I32, (256, 512), 1)
        cc = jnp.where(row >= (c0 + 1) * V, c0 + 1, c0)
        dd = row - cc * V
        of_c = look_up(jnp.where(orb == cc, F32(1), F32(0)).astype(BF16), table, ((1,), (1,)))
        of_d = look_up(jnp.where(orb == dd, F32(1), F32(0)).astype(BF16), table, ((1,), (1,)))
        row = row[:, 0:128]
        inside = (row >= ROWS * p) & (row < ROWS * p + ROWS)
        rowirr[pl.ds(pl.multiple_of(t * 256, 256), 256), :] = jnp.where(inside, of_c ^ of_d, -1)
        return carry

    lax.fori_loop(0, LANES // 256, fill_rows, 0)

    for k, (offset, size) in enumerate(CHUNKS):
        settle(bbuf[k].at[pl.ds(0, 3), pl.ds(0, size // 8)], b_recv.at[k])
        own[2 * k].wait()

        def mask(t, carry):
            rows = pl.multiple_of(t * 128, 128)
            row_irrep = rowirr[pl.ds(offset + rows, 128), :]
            for block in range(8):
                slab, half = block // 2, block % 2
                part = bbuf[k][slab, pl.ds(MARGIN + t * 16, 16), :, pl.ds(half * 128, 128)]
                part = part.astype(F32).reshape(128, 128)
                keep = row_irrep == colirr[0:1, block * 128:block * 128 + 128]
                bm[pl.ds(rows, 128), block * 128:block * 128 + 128] = jnp.where(
                    keep, part, F32(0)
                ).astype(BF16)
            bp[pl.ds(rows, 128), :] = jnp.dot(
                bm[pl.ds(rows, 128), :], perm[...], preferred_element_type=F32
            ).astype(BF16)
            return carry

        lax.fori_loop(0, size // 128, mask, 0)
        settle(abuf[k].at[pl.ds(0, 31)], a_recv.at[k])
        own[2 * k + 1].wait()

        def multiply(t, carry):
            left = abuf[k][pl.ds(t * 8, 8)].reshape(256, size)
            for slab in range(NZ):
                cols = slice(slab * 256, slab * 256 + 256)
                direct = jnp.dot(left, bm[0:size, cols], preferred_element_type=F32)
                direct = direct.reshape(4, 2, 32, 256)
                mirror = jnp.dot(left, bp[0:size, cols], preferred_element_type=F32)
                rows = pl.ds(pl.multiple_of(t * 256, 256), 256)
                if k:
                    c_ref[slab, t] += direct
                    d_ref[2 * slab, rows] += mirror[:, 0:128]
                    d_ref[2 * slab + 1, rows] += mirror[:, 128:256]
                else:
                    c_ref[slab, t] = direct
                    d_ref[2 * slab, rows] = mirror[:, 0:128]
                    d_ref[2 * slab + 1, rows] = mirror[:, 128:256]
            return carry

        lax.fori_loop(0, 4, multiply, 0)

    merges = []
    sibling = pair_at(0, 0, 1)
    for slab in range(NZ):
        def join(m, carry):
            for core in range(2):
                for half in range(2):
                    mirrored = d_ref[2 * slab + half, pl.ds(2 * m + core, 32, stride=32), :]
                    c_ref[slab, m // 4, lax.rem(m, 4), core, :, half * 128:half * 128 + 128] += mirrored
            return carry

        lax.fori_loop(0, 16, join, 0)
        merges.append(
            remote(
                c_ref.at[slab, :, :, 1 - c], r_ref.at[slab], m_send.at[slab], m_recv.at[slab],
                sibling, s,
            )
        )
        merges[-1].start()
    for slab in range(NZ):
        merges[slab].wait_recv()

        def merge(m, carry):
            r_ref[slab, m // 4, lax.rem(m, 4)] += c_ref[slab, m // 4, lax.rem(m, 4), c]
            return carry

        lax.fori_loop(0, 16, merge, 0)

    place = {"z": s, "x": x, "y": y}

    for step in range(3):
        for part, (row, rows, lane, lanes, order) in enumerate(PARTS):
            axis = order[step]
            done = order[:step]
            for d in (1, 3, 2):
                target = shift(place[axis], d, 4)
                fixed = {a: place[a] for a in done}
                fixed[axis] = target
                index = tuple(
                    fixed[a] if a in fixed else slice(None) for a in ("z", "x", "y")
                )
                peer = p
                slab = s
                if axis == "x":
                    peer = target * 8 + y * 2 + c
                elif axis == "y":
                    peer = x * 8 + target * 2 + c
                else:
                    slab = target
                remote(
                    r5_at(r_ref, index, row, rows, lane, lanes),
                    q[3 * part + step].at[d - 1],
                    q_send.at[part, step], q_recv.at[part, step], peer, slab,
                ).start()
        for part, (row, rows, lane, lanes, order) in enumerate(PARTS):
            buffer = q[3 * part + step]
            settle(buffer, q_recv.at[part, step])
            fixed = {a: place[a] for a in order[:step + 1]}
            free = [a for a in ("z", "x", "y") if a not in fixed]

            def add(t, carry):
                spots = {}
                rest = t
                for a in reversed(free):
                    spots[a] = lax.rem(rest, 4)
                    rest = rest // 4
                where = tuple(fixed[a] if a in fixed else spots[a] for a in ("z", "x", "y"))
                spot = tuple(spots[a] for a in free)
                mine = r5_at(r_ref, where, row, rows, lane, lanes)
                total = mine[...]
                for d in range(3):
                    total = total + buffer[(d, *spot)]
                if step == 2:
                    out[pl.ds(row, rows), pl.ds(lane, lanes)] = total
                else:
                    mine[...] = total
                return carry

            if free:
                lax.fori_loop(0, 4 ** len(free), add, 0)
            else:
                add(0, 0)

    for k in range(nk):
        settle(abuf[k].at[pl.ds(0, 31)], a_send)
        settle(bbuf[k].at[pl.ds(0, 3), pl.ds(0, CHUNKS[k][1] // 8)], b_send)
    for slab in range(NZ):
        merges[slab].wait_send()
    for part in range(3):
        for step in range(3):
            settle(q[3 * part + step], q_send.at[part, step])


def r5_at(ref, index, row, rows, lane, lanes):
    z, x, y = index
    return ref.at[z, x, y, pl.ds(row, rows), pl.ds(lane, lanes)]


def contract(amps, ints, irrep):
    nk = len(CHUNKS)
    dma = pltpu.SemaphoreType.DMA
    scratch = [pltpu.VMEM((OCC, 32, size), BF16) for _, size in CHUNKS]
    scratch += [pltpu.VMEM((NZ, size // 8 + 2 * MARGIN, 8, 256), BF16) for _, size in CHUNKS]
    widest = max(size for _, size in CHUNKS)
    scratch += [
        pltpu.VMEM((widest, 1024), BF16),
        pltpu.VMEM((widest, 1024), BF16),
        pltpu.VMEM((1024, 1024), BF16),
        pltpu.VMEM((8, 512), F32),
        pltpu.VMEM((LANES, 128), I32),
        pltpu.VMEM((8, 1024), I32),
        pltpu.VMEM((NZ, 4, 4, 2, 32, 256), F32),
        pltpu.VMEM((2 * NZ, 1024, 128), F32),
        pltpu.VMEM((NZ, 4, 4, 32, 256), F32),
    ]
    for row, rows, lane, lanes, _ in PARTS:
        for dims in STEP_DIMS:
            scratch.append(pltpu.VMEM((3, *dims, rows, lanes), F32))
    scratch += [
        dma, dma, dma((nk,)), dma((nk,)), dma((nk, 2)), dma((NZ,)), dma((NZ,)), dma((3, 3)), dma((3, 3)),
    ]
    return pl.pallas_call(
        kernel,
        out_shape=jax.ShapeDtypeStruct((32, 256), F32),
        in_specs=[
            pl.BlockSpec(memory_space=pltpu.HBM),
            pl.BlockSpec(memory_space=pltpu.HBM),
            pl.BlockSpec(memory_space=pltpu.VMEM),
        ],
        out_specs=pl.BlockSpec(memory_space=pltpu.VMEM),
        scratch_shapes=scratch,
        compiler_params=pltpu.CompilerParams(
            collective_id=0, has_side_effects=True, vmem_limit_bytes=52 << 20
        ),
    )(amps, ints, irrep)


def local(amplitudes, integrals, virt_irrep, occ_energy, slab_energy):
    pair_index = lax.axis_index("pair")
    slab_index = lax.axis_index("slab")
    summed = contract(
        amplitudes.reshape(OCC, V * V), integrals.reshape(GROUPS, 8, 256), virt_irrep.reshape(1, V)
    )
    symmetric = summed.reshape(1, OCC, VS // NZ, VS)
    energy_i = lax.dynamic_slice_in_dim(occ_energy, pair_index, 1, 0)
    energy_a = lax.dynamic_slice_in_dim(slab_energy, slab_index * (VS // NZ), VS // NZ, 0)
    denominator = (
        energy_a[None, None, :, None]
        + slab_energy[None, None, None, :]
        - energy_i[:, None, None, None]
        - occ_energy[None, :, None, None]
    )
    return symmetric / denominator


def solution(mesh):
    placed = (P("pair", None, None), P("pair", "slab"), P(), P(), P())
    return jax.shard_map(
        local, mesh=mesh, in_specs=placed, out_specs=P("pair", None, "slab", None), check_vma=False
    )
```

time: 1620 us -> 70.9 us (0.04); the launches traced: 1600 us -> 70.8 us
  other arithmetic: 873 us -> 1.48 us
  local copies, waits for them, and re-layouts: 434 us -> 1.46 us
  waiting for transfers between devices: 249 us -> 0 us
  Pallas kernels: 0 us -> 67.8 us
  starting transfers between devices: 17.5 us -> 0 us
    unnamed x1 -> x0, other arithmetic: 871 us -> none
    unnamed x15 -> x6, local copies, waits for them, and re-layouts: 246 us -> 0.72 us
    all_to_all x8 -> x0, local copies, waits for them, and re-layouts: 183 us -> none  [the longest x3 183 us: local(): lax.all_to_all(amplitudes, 'pair', split_axis=2, concat_axis=0, tiled=True)]
    all_to_all x3 -> x0, waiting for transfers between devices: 151 us -> none  [the longest x1 140 us: local(): lax.all_to_all(amplitudes, 'pair', split_axis=2, concat_axis=0, tiled=True)]
    reduce_scatter x1 -> x0, waiting for transfers between devices: 97.9 us -> none  [local(): lax.psum_scatter(product.reshape(count, occupied, cols_local), 'pair', sc...]
    pallas_call x0 -> x1, Pallas kernels: none -> 67.8 us  [contract(): pl.pallas_call(kernel, out_shape=jax.ShapeDtypeStruct((32, 256), F32), in...]
    all_to_all x3 -> x0, starting transfers between devices: 17.3 us -> none  [the longest x1 7.65 us: local(): lax.all_to_all(amplitudes, 'pair', split_axis=2, concat_axis=0, tiled=True)]
  transfers between devices with their start and end apart: 4 -> 0, of which waited for: 4 -> 0; matrix products, arithmetic and copies ran while one was open for 0% -> 0% of each run, Pallas kernels for 0% -> 0%
where the time goes in v1:
time: 70.9 us; the launch traced here: 70.8 us
  Pallas kernels  67.8 us (96%)
  other arithmetic  1.48 us (2%)
  local copies, waits for them, and re-layouts  1.46 us (2%)
    pallas_call x1, Pallas kernels, contract(): pl.pallas_call(kernel, out_shape=jax.ShapeDtypeStruct((32, 256), F32), in...  67.8 us

profile of v1, /device:TPU:0, one launch (start us, length us, event | category | flops | bytes accessed | tf_op | source)
XLA Modules:
  0.0 70.8 jit_solution(8956555710032598842)
XLA Ops:
  0.0 0.0 copy-start.1
  0.0 0.0 copy-start.2
  0.0 0.0 copy-start
  0.0 0.7 copy-done
  0.7 67.8 %shard_map.55 = f32[32,256]{1,0:T(8,128)S(1)} custom-call(bf16[32,160000]{1,0:T(8,128)(2,1)} %bitcast.5, bf16[625,8,256]{2,1,0:T(8,128)(2,1)} %bitcast.6, s32[1,400]{1,0:T(1,128)S(1)} %bitcast.4), custom_call_target="tpu_custom_call" | custom-call | tf_op jit(solution)/shard_map/pallas_call | solution.py:320
  68.6 0.1 reshape.73
  68.7 0.0 copy-done.1
  68.7 0.6 dynamic_slice.7
  69.3 0.0 copy-done.2
  69.3 0.1 dynamic_slice.6
  69.3 0.7 %add_subtract_fusion = f32[8,32]{1,0:T(8,128)S(1)} fusion(f32[]{:T(128)} %bitcast.3, f32[32]{0:T(128)S(1)} %copy-done.2, f32[8]{0:T(128)S(1)} %dynamic_slice.6), kind=kLoop, calls=%fused_computation.1 | loop fusion | flops 512 | bytes 1188 | tf_op jit(solution)/shard_map/sub | solution.py:346
  70.0 0.8 %subtract_divide_fusion = f32[1,32,8,32]{3,2,1,0:T(8,128)} fusion(f32[1,32,8,32]{3,2,1,0:T(8,128)S(1)} %reshape.73, f32[32]{0:T(128)S(1)} %copy-done.1, f32[8,32]{1,0:T(8,128)S(1)} %add_subtract_fusion), kind=kLoop, calls=%fused_computation | loop fusion | flops 16384 | bytes 66688 | tf_op jit(solution)/shard_map/div | solution.py:351
Async XLA Ops:
  0.0 68.7 %copy-start.1 = (f32[32]{0:T(128)S(1)}, f32[32]{0:T(128)}, u32[]{:S(2)}) copy-start(f32[32]{0:T(128)} %param.8) | copy-start | bytes 388
  0.0 69.3 %copy-start.2 = (f32[32]{0:T(128)S(1)}, f32[32]{0:T(128)}, u32[]{:S(2)}) copy-start(f32[32]{0:T(128)} %param.9) | copy-start | bytes 388
  0.0 0.7 %copy-start = (s32[400]{0:T(512)S(1)}, s32[400]{0:T(512)}, u32[]{:S(2)}) copy-start(s32[400]{0:T(512)} %param.7) | copy-start | bytes 4804

commit v2 on v1

v2 whole, which is shorter than its diff:
```python
import jax
import jax.numpy as jnp
from jax import lax
from jax.experimental import pallas as pl
from jax.experimental.pallas import tpu as pltpu
from jax.sharding import PartitionSpec as P

F32, BF16, I32 = jnp.float32, jnp.bfloat16, jnp.int32
V, VS, OCC = 400, 32, 32
NZ = 4
ROWS = 5000
GROUPS = ROWS // 8
LANES = 1280
CHUNKS = ((0, 512), (512, 512), (1024, 256))
MARGIN = 16
PARTS = (
    (0, 24, 0, 128, ("z", "x", "y")),
    (0, 24, 128, 128, ("x", "y", "z")),
    (24, 8, 0, 256, ("y", "z", "x")),
)
STEP_DIMS = ((4, 4), (4,), ())
AXES = ("z", "x", "y")


def shift(i, d, n):
    return lax.rem(i + d, n)


def remote(src, dst, send, recv, pair, slab):
    return pltpu.make_async_remote_copy(
        src_ref=src, dst_ref=dst, send_sem=send, recv_sem=recv,
        device_id={"pair": pair, "slab": slab}, device_id_type=pl.DeviceIdType.MESH,
    )


def settle(ref, sem):
    pltpu.make_async_copy(ref, ref, sem).wait()


def one_hot(test):
    return jnp.where(test, F32(1), F32(0)).astype(BF16)


def kernel(amps, ints, irrep, occ, virt, out, *refs):
    nk = len(CHUNKS)
    abuf, bbuf = refs[:nk], refs[nk:2 * nk]
    refs = refs[2 * nk:]
    ap, bm, bp, perm, vrow, rowirr, colirr, den, fin, c_ref, r_ref = refs[:11]
    irrep_v, occ_s, virt_s = refs[11:14]
    q = refs[14:23]
    a_send, b_send, a_recv, b_recv, own_sem, arg_sem, m_send, m_recv, q_send, q_recv = refs[23:]

    p = lax.axis_index("pair")
    s = lax.axis_index("slab")
    x, y, c = p // 8, lax.rem(p // 2, 4), lax.rem(p, 2)
    place = {"z": s, "x": x, "y": y}

    def pair_at(dx, dy, dc):
        return shift(x, dx, 4) * 8 + shift(y, dy, 4) * 2 + shift(c, dc, 2)

    barrier = pltpu.get_barrier_semaphore()

    def greet(pair, slab):
        pl.semaphore_signal(
            barrier, inc=1, device_id={"pair": pair, "slab": slab},
            device_id_type=pl.DeviceIdType.MESH,
        )

    def greet_some(i, carry):
        for dx in (2, 1, 3, 0):
            greet(pair_at(dx, i // 2 + dx, lax.rem(i, 2)), s)
        return carry

    for dx in (2, 1, 3):
        greet(pair_at(dx, dx, 0), s)
    lax.fori_loop(1, 8, greet_some, 0)
    for dz in (2, 1, 3):
        greet(p, shift(s, dz, NZ))
    small = [
        pltpu.make_async_copy(src, dst, arg_sem.at[i])
        for i, (src, dst) in enumerate(((irrep, irrep_v), (occ, occ_s), (virt, virt_s)))
    ]
    for copy in small:
        copy.start()
    pl.semaphore_wait(barrier, 34)

    first_tile = ROWS * p // 128
    lead = lax.rem(p, 16)

    def columns(pair, k):
        tile = ROWS * pair // 128 + 10 * s
        return pl.ds(pl.multiple_of(tile * 128 + CHUNKS[k][0], 128), CHUNKS[k][1])

    def rows_for(slab, k):
        size = CHUNKS[k][1] // 8
        want = 160 * slab - lead + CHUNKS[k][0] // 8
        have = jnp.clip(want, 0, GROUPS - size)
        return pl.ds(have, size), pl.ds(MARGIN + have - want, size)

    def send_amps(k, dx, dy, dc):
        peer = pair_at(dx, dy, dc)
        remote(
            amps.at[:, columns(peer, k)], abuf[k].at[p], a_send, a_recv.at[k], peer, s
        ).start()

    own = []
    for k in range(nk):
        for dz in (1, 3, 2):
            slab = shift(s, dz, NZ)
            source, target = rows_for(slab, k)
            remote(
                ints.at[source], bbuf[k].at[s, target], b_send, b_recv.at[k], p, slab
            ).start()
        source, target = rows_for(s, k)
        own.append(pltpu.make_async_copy(ints.at[source], bbuf[k].at[s, target], own_sem.at[k, 0]))
        own.append(pltpu.make_async_copy(amps.at[:, columns(p, k)], abuf[k].at[p], own_sem.at[k, 1]))
        for dx in (1, 3, 2):
            send_amps(k, dx, dx, 0)

        def send_some(i, carry):
            for dx in (1, 3, 2, 0):
                send_amps(k, dx, i // 2 + dx, lax.rem(i, 2))
            return carry

        lax.fori_loop(1, 8, send_some, 0)
    for copy in own:
        copy.start()

    def fill_perm(t, carry):
        row = lax.broadcasted_iota(I32, (128, 1024), 0) + t * 128
        col = lax.broadcasted_iota(I32, (128, 1024), 1)
        swapped = ((row & 31) << 5) | (row >> 5)
        perm[pl.ds(pl.multiple_of(t * 128, 128), 128), :] = one_hot(swapped == col)
        return carry

    lax.fori_loop(0, 8, fill_perm, 0)
    for copy in small:
        copy.wait()

    vrow[...] = jnp.zeros_like(vrow)
    vrow[0:1, 0:V] = irrep_v[...].astype(F32)
    table = jnp.broadcast_to(vrow[0:1, :], (128, 512)).astype(BF16)

    def look_up(lhs, rhs, dims):
        return lax.dot_general(
            lhs, rhs, (dims, ((), ())), preferred_element_type=F32
        ).astype(I32)

    orb = lax.broadcasted_iota(I32, (128, 1024), 0)
    col = lax.broadcasted_iota(I32, (128, 1024), 1)
    first = table[0:16, 0:128]
    of_a = look_up(first, one_hot(orb == (col >> 5)), ((1,), (0,)))
    of_b = look_up(first, one_hot(orb == (col & 31)), ((1,), (0,)))
    colirr[...] = (of_a ^ of_b)[0:8]

    start = (first_tile + 10 * s) * 128

    def fill_rows(t, carry):
        base = start + t * 256
        c0 = base // V
        row = lax.broadcasted_iota(I32, (256, 512), 0) + base
        orb = lax.broadcasted_iota(I32, (256, 512), 1)
        cc = jnp.where(row >= (c0 + 1) * V, c0 + 1, c0)
        of_c = look_up(one_hot(orb == cc), table, ((1,), (1,)))
        of_d = look_up(one_hot(orb == row - cc * V), table, ((1,), (1,)))
        row = row[:, 0:128]
        inside = (row >= ROWS * p) & (row < ROWS * p + ROWS)
        rowirr[pl.ds(pl.multiple_of(t * 256, 256), 256), :] = jnp.where(inside, of_c ^ of_d, -1)
        return carry

    lax.fori_loop(0, LANES // 256, fill_rows, 0)

    lane = lax.broadcasted_iota(I32, (8, 256), 1)
    row = lax.broadcasted_iota(I32, (32, 256), 0)
    of_a = jnp.zeros((8, 256), F32)
    of_b = jnp.zeros((8, 256), F32)
    of_j = jnp.zeros((32, 256), F32)
    for i in range(VS // NZ):
        of_a = jnp.where((lane >> 5) == i, virt_s[0, s * (VS // NZ) + i], of_a)
    for i in range(VS):
        of_b = jnp.where((lane & 31) == i, virt_s[0, i], of_b)
    for i in range(OCC):
        of_j = jnp.where(row == i, occ_s[0, i], of_j)
    den[...] = ((of_a + of_b) - occ_s[0, p])[0:1] - of_j

    merges = []
    sibling = pair_at(0, 0, 1)
    for k, (offset, size) in enumerate(CHUNKS):
        settle(bbuf[k].at[pl.ds(0, 3), pl.ds(0, size // 8)], b_recv.at[k])
        own[2 * k].wait()

        def mask(t, carry):
            rows = pl.multiple_of(t * 128, 128)
            row_irrep = rowirr[pl.ds(offset + rows, 128), :]
            for block in range(8):
                slab, half = block // 2, block % 2
                part = bbuf[k][slab, pl.ds(MARGIN + t * 16, 16), :, pl.ds(half * 128, 128)]
                part = part.astype(F32).reshape(128, 128)
                keep = row_irrep == colirr[0:1, block * 128:block * 128 + 128]
                bm[pl.ds(rows, 128), block * 128:block * 128 + 128] = jnp.where(
                    keep, part, F32(0)
                ).astype(BF16)
            bp[pl.ds(rows, 128), :] = jnp.dot(
                bm[pl.ds(rows, 128), :], perm[...], preferred_element_type=F32
            ).astype(BF16)
            return carry

        lax.fori_loop(0, size // 128, mask, 0)
        settle(abuf[k].at[pl.ds(0, 31)], a_recv.at[k])
        own[2 * k + 1].wait()

        def mirror(t, carry):
            rows = pl.ds(pl.multiple_of(t * 256, 256), 256)
            ap[rows, 0:size] = jnp.dot(
                perm[rows, :], abuf[k][...].reshape(1024, size), preferred_element_type=F32
            ).astype(BF16)
            return carry

        lax.fori_loop(0, 4, mirror, 0)

        def multiply(t, slab):
            cols = pl.ds(pl.multiple_of(slab * 256, 256), 256)
            direct = jnp.dot(
                abuf[k][pl.ds(t * 8, 8)].reshape(256, size), bm[0:size, cols],
                preferred_element_type=F32,
            )
            swapped = jnp.dot(
                ap[pl.ds(pl.multiple_of(t * 256, 256), 256), 0:size], bp[0:size, cols],
                preferred_element_type=F32,
            )
            total = (direct + swapped).reshape(4, 2, 32, 256)
            if k:
                total = total + c_ref[slab, t]
            c_ref[slab, t] = total
            return slab

        if k < nk - 1:
            def multiply_all(i, carry):
                multiply(i // 4, lax.rem(i, 4))
                return carry

            lax.fori_loop(0, 16, multiply_all, 0)
        else:
            for n, dz in enumerate((2, 1, 3, 0)):
                slab = shift(s, dz, NZ)
                lax.fori_loop(0, 4, multiply, slab)
                merges.append(
                    remote(
                        c_ref.at[slab, :, :, 1 - c], r_ref.at[slab], m_send.at[n], m_recv.at[n],
                        sibling, s,
                    )
                )
                merges[-1].start()

    def block(index, part):
        row, rows, lane, lanes, _ = PARTS[part]
        return r_ref.at[(*index, pl.ds(row, rows), pl.ds(lane, lanes))]

    def hand_on(part, step, d, index, target, extra=()):
        axis = PARTS[part][4][step]
        at = {**place, axis: target}
        remote(
            block(index, part), q[3 * part + step].at[(d - 1, *extra)],
            q_send.at[part, step], q_recv.at[part, step],
            at["x"] * 8 + at["y"] * 2 + c, at["z"],
        ).start()

    every = slice(None)
    for n, dz in enumerate((2, 1, 3, 0)):
        slab = shift(s, dz, NZ)
        merges[n].wait_recv()

        def merge(m, carry):
            r_ref[slab, m // 4, lax.rem(m, 4)] += c_ref[slab, m // 4, lax.rem(m, 4), c]
            return carry

        lax.fori_loop(0, 16, merge, 0)
        if dz:
            hand_on(0, 0, dz, (slab, every, every), slab)
        for d in (1, 3, 2):
            target = shift(x, d, 4)
            hand_on(1, 0, d, (slab, target, every), target, (slab,))
            target = shift(y, d, 4)
            hand_on(2, 0, d, (slab, every, target), target, (slab,))

    for step in range(3):
        for part, (row, rows, lane, lanes, order) in enumerate(PARTS):
            buffer = q[3 * part + step]
            settle(buffer, q_recv.at[part, step])
            fixed = {a: place[a] for a in order[:step + 1]}
            free = [a for a in AXES if a not in fixed]

            def add(t, carry):
                spots = {}
                rest = t
                for a in reversed(free):
                    spots[a] = lax.rem(rest, 4)
                    rest = rest // 4
                mine = block([fixed[a] if a in fixed else spots[a] for a in AXES], part)
                total = mine[...]
                for d in range(3):
                    total = total + buffer[(d, *[spots[a] for a in free])]
                if step == 2:
                    fin[pl.ds(row, rows), pl.ds(lane, lanes)] = total
                else:
                    mine[...] = total
                return carry

            if free:
                lax.fori_loop(0, 4 ** len(free), add, 0)
            else:
                add(0, 0)
            if step < 2:
                axis = order[step + 1]
                for d in (1, 3, 2):
                    target = shift(place[axis], d, 4)
                    at = {**fixed, axis: target}
                    hand_on(part, step + 1, d, tuple(at.get(a, every) for a in AXES), target)

    fin[...] = fin[...] / den[...]
    for i in range(VS // NZ):
        out[pl.ds(i, 32, stride=VS // NZ), :] = fin[:, i * VS:i * VS + VS]

    for k in range(nk):
        settle(abuf[k].at[pl.ds(0, 31)], a_send)
        settle(bbuf[k].at[pl.ds(0, 3), pl.ds(0, CHUNKS[k][1] // 8)], b_send)
    for n in range(NZ):
        merges[n].wait_send()
    for part in range(3):
        for step in range(3):
            settle(q[3 * part + step], q_send.at[part, step])


def contract(amps, ints, irrep, occ, virt):
    nk = len(CHUNKS)
    dma = pltpu.SemaphoreType.DMA
    widest = max(size for _, size in CHUNKS)
    scratch = [pltpu.VMEM((OCC, 32, size), BF16) for _, size in CHUNKS]
    scratch += [pltpu.VMEM((NZ, size // 8 + 2 * MARGIN, 8, 256), BF16) for _, size in CHUNKS]
    scratch += [
        pltpu.VMEM((1024, widest), BF16),
        pltpu.VMEM((widest, 1024), BF16),
        pltpu.VMEM((widest, 1024), BF16),
        pltpu.VMEM((1024, 1024), BF16),
        pltpu.VMEM((8, 512), F32),
        pltpu.VMEM((LANES, 128), I32),
        pltpu.VMEM((8, 1024), I32),
        pltpu.VMEM((32, 256), F32),
        pltpu.VMEM((32, 256), F32),
        pltpu.VMEM((NZ, 4, 4, 2, 32, 256), F32),
        pltpu.VMEM((NZ, 4, 4, 32, 256), F32),
        pltpu.VMEM((1, V), I32),
        pltpu.SMEM((1, OCC), F32),
        pltpu.SMEM((1, VS), F32),
    ]
    for _, rows, _, lanes, _ in PARTS:
        for dims in STEP_DIMS:
            scratch.append(pltpu.VMEM((3, *dims, rows, lanes), F32))
    scratch += [
        dma, dma, dma((nk,)), dma((nk,)), dma((nk, 2)), dma((3,)), dma((NZ,)), dma((NZ,)),
        dma((3, 3)), dma((3, 3)),
    ]
    return pl.pallas_call(
        kernel,
        out_shape=jax.ShapeDtypeStruct((OCC * VS // NZ, VS), F32),
        in_specs=[pl.BlockSpec(memory_space=pltpu.HBM)] * 5,
        out_specs=pl.BlockSpec(memory_space=pltpu.VMEM),
        scratch_shapes=scratch,
        compiler_params=pltpu.CompilerParams(
            collective_id=0, has_side_effects=True, vmem_limit_bytes=52 << 20
        ),
    )(amps, ints, irrep, occ, virt)


def local(amplitudes, integrals, virt_irrep, occ_energy, slab_energy):
    update = contract(
        amplitudes.reshape(OCC, V * V), integrals.reshape(GROUPS, 8, 256),
        virt_irrep.reshape(1, V), occ_energy.reshape(1, OCC), slab_energy.reshape(1, VS),
    )
    return update.reshape(1, OCC, VS // NZ, VS)


def solution(mesh):
    placed = (P("pair", None, None), P("pair", "slab"), P(), P(), P())
    return jax.shard_map(
        local, mesh=mesh, in_specs=placed, out_specs=P("pair", None, "slab", None), check_vma=False
    )
```

time: 70.9 us -> 71.7 us (1.011)
  other arithmetic: 1.48 us -> 0 us
  local copies, waits for them, and re-layouts: 1.46 us -> 2.65 us
  Pallas kernels: 67.8 us -> 68.7 us
    unnamed x6 -> x7, local copies, waits for them, and re-layouts: 0.72 us -> 2.65 us
    pallas_call x1, Pallas kernels: 67.8 us -> 68.7 us  [contract(): pl.pallas_call(kernel, out_shape=jax.ShapeDtypeStruct((OCC * VS // NZ, VS...]
    div x1 -> x0, other arithmetic: 0.77 us -> none  [local(): return symmetric / denominator]
where the time goes in v2:
time: 71.7 us; the launch traced here: 71.3 us
  Pallas kernels  68.7 us (96%)
  local copies, waits for them, and re-layouts  2.65 us (4%)
    pallas_call x1, Pallas kernels, contract(): pl.pallas_call(kernel, out_shape=jax.ShapeDtypeStruct((OCC * VS // NZ, VS...  68.7 us
    unnamed x7, local copies, waits for them, and re-layouts  2.65 us

profile of v2, /device:TPU:0, one launch (start us, length us, event | category | flops | bytes accessed | tf_op | source)
XLA Modules:
  0.0 71.3 jit_solution(6465874513373711374)
XLA Ops:
  0.0 0.0 copy-start
  0.0 0.7 copy-done
  0.7 0.0 copy-start.1
  0.7 0.7 copy-done.1
  1.3 0.0 copy-start.2
  1.3 0.7 copy-done.2
  2.0 68.7 %shard_map.55 = f32[256,32]{1,0:T(8,128)S(1)} custom-call(bf16[32,160000]{1,0:T(8,128)(2,1)} %bitcast.10, bf16[625,8,256]{2,1,0:T(8,128)(2,1)} %bitcast.11, s32[1,400]{1,0:T(1,128)S(1)} %bitcast.7, f32[1,32]{1,0:T(1,128)S(1)} %bitcast.8, f32[1,32]{1,0:T(1,128)S(1)} %bitcast.9), custom_call_target="tpu_custom_call" | custom-call | tf_op jit(solution)/shard_map/pallas_call | solution.py:363
  70.7 0.7 copy.7
Async XLA Ops:
  0.0 0.7 copy-start
  0.7 0.7 copy-start.1
  1.3 0.7 copy-start.2

commit v3 on v2

--- a/solution.py
+++ b/solution.py
@@ -45,10 +45,10 @@
     nk = len(CHUNKS)
     abuf, bbuf = refs[:nk], refs[nk:2 * nk]
     refs = refs[2 * nk:]
-    ap, bm, bp, perm, vrow, rowirr, colirr, den, fin, c_ref, r_ref = refs[:11]
-    irrep_v, occ_s, virt_s = refs[11:14]
-    q = refs[14:23]
-    a_send, b_send, a_recv, b_recv, own_sem, arg_sem, m_send, m_recv, q_send, q_recv = refs[23:]
+    ap, bm, bp, perm_ij, perm_ab, vrow, rowirr, colirr, den, fin, c_ref, r_ref = refs[:12]
+    irrep_v, occ_s, virt_s = refs[12:15]
+    q = refs[15:24]
+    a_send, b_send, a_recv, b_recv, own_sem, arg_sem, m_send, m_recv, q_send, q_recv = refs[24:]
 
     p = lax.axis_index("pair")
     s = lax.axis_index("slab")
@@ -109,10 +109,10 @@
             slab = shift(s, dz, NZ)
             source, target = rows_for(slab, k)
             remote(
-                ints.at[source], bbuf[k].at[s, target], b_send, b_recv.at[k], p, slab
+                ints.at[source], bbuf[k].at[3 - dz, target], b_send, b_recv.at[k], p, slab
             ).start()
         source, target = rows_for(s, k)
-        own.append(pltpu.make_async_copy(ints.at[source], bbuf[k].at[s, target], own_sem.at[k, 0]))
+        own.append(pltpu.make_async_copy(ints.at[source], bbuf[k].at[3, target], own_sem.at[k, 0]))
         own.append(pltpu.make_async_copy(amps.at[:, columns(p, k)], abuf[k].at[p], own_sem.at[k, 1]))
         for dx in (1, 3, 2):
             send_amps(k, dx, dx, 0)
@@ -126,11 +126,18 @@
     for copy in own:
         copy.start()
 
+    def orbitals(col):
+        return ((((col >> 8) + s + 1) & 3) << 3) | ((col >> 5) & 7), col & 31
+
     def fill_perm(t, carry):
         row = lax.broadcasted_iota(I32, (128, 1024), 0) + t * 128
         col = lax.broadcasted_iota(I32, (128, 1024), 1)
-        swapped = ((row & 31) << 5) | (row >> 5)
-        perm[pl.ds(pl.multiple_of(t * 128, 128), 128), :] = one_hot(swapped == col)
+        rows = pl.ds(pl.multiple_of(t * 128, 128), 128)
+        perm_ij[rows, :] = one_hot((((row & 31) << 5) | (row >> 5)) == col)
+        a, b = orbitals(col)
+        perm_ab[rows, :] = one_hot(
+            row == (((((b >> 3) + 3 - s) & 3) << 8) | ((b & 7) << 5) | a)
+        )
         return carry
 
     lax.fori_loop(0, 8, fill_perm, 0)
@@ -149,8 +156,7 @@
     orb = lax.broadcasted_iota(I32, (128, 1024), 0)
     col = lax.broadcasted_iota(I32, (128, 1024), 1)
     first = table[0:16, 0:128]
-    of_a = look_up(first, one_hot(orb == (col >> 5)), ((1,), (0,)))
-    of_b = look_up(first, one_hot(orb == (col & 31)), ((1,), (0,)))
+    of_a, of_b = (look_up(first, one_hot(orb == v), ((1,), (0,))) for v in orbitals(col))
     colirr[...] = (of_a ^ of_b)[0:8]
 
     start = (first_tile + 10 * s) * 128
@@ -201,7 +207,7 @@
                     keep, part, F32(0)
                 ).astype(BF16)
             bp[pl.ds(rows, 128), :] = jnp.dot(
-                bm[pl.ds(rows, 128), :], perm[...], preferred_element_type=F32
+                bm[pl.ds(rows, 128), :], perm_ab[...], preferred_element_type=F32
             ).astype(BF16)
             return carry
 
@@ -212,82 +218,83 @@
         def mirror(t, carry):
             rows = pl.ds(pl.multiple_of(t * 256, 256), 256)
             ap[rows, 0:size] = jnp.dot(
-                perm[rows, :], abuf[k][...].reshape(1024, size), preferred_element_type=F32
+                perm_ij[rows, :], abuf[k][...].reshape(1024, size), preferred_element_type=F32
             ).astype(BF16)
             return carry
 
         lax.fori_loop(0, 4, mirror, 0)
 
-        def multiply(t, slab):
-            cols = pl.ds(pl.multiple_of(slab * 256, 256), 256)
+        def multiply(t, n):
+            cols = slice(n * 256, n * 256 + 256)
             direct = jnp.dot(
                 abuf[k][pl.ds(t * 8, 8)].reshape(256, size), bm[0:size, cols],
                 preferred_element_type=F32,
             )
+            rows = t * 256 if isinstance(t, int) else pl.multiple_of(t * 256, 256)
             swapped = jnp.dot(
-                ap[pl.ds(pl.multiple_of(t * 256, 256), 256), 0:size], bp[0:size, cols],
-                preferred_element_type=F32,
+                ap[pl.ds(rows, 256), 0:size], bp[0:size, cols], preferred_element_type=F32
             )
             total = (direct + swapped).reshape(4, 2, 32, 256)
             if k:
-                total = total + c_ref[slab, t]
-            c_ref[slab, t] = total
-            return slab
+                total = total + c_ref[n, t]
+            c_ref[n, t] = total
 
         if k < nk - 1:
-            def multiply_all(i, carry):
-                multiply(i // 4, lax.rem(i, 4))
+            def multiply_all(t, carry):
+                for n in range(NZ):
+                    multiply(t, n)
                 return carry
 
-            lax.fori_loop(0, 16, multiply_all, 0)
+            lax.fori_loop(0, 4, multiply_all, 0)
         else:
-            for n, dz in enumerate((2, 1, 3, 0)):
-                slab = shift(s, dz, NZ)
-                lax.fori_loop(0, 4, multiply, slab)
+            for n in range(NZ):
+                for t in range(4):
+                    multiply(t, n)
                 merges.append(
                     remote(
-                        c_ref.at[slab, :, :, 1 - c], r_ref.at[slab], m_send.at[n], m_recv.at[n],
+                        c_ref.at[n, :, :, 1 - c], r_ref.at[n], m_send.at[n], m_recv.at[n],
                         sibling, s,
                     )
                 )
                 merges[-1].start()
 
+    own_at = {"z": 3, "x": x, "y": y}
+
     def block(index, part):
         row, rows, lane, lanes, _ = PARTS[part]
         return r_ref.at[(*index, pl.ds(row, rows), pl.ds(lane, lanes))]
 
-    def hand_on(part, step, d, index, target, extra=()):
+    def hand_on(part, step, d, fixed, extra=()):
         axis = PARTS[part][4][step]
+        target = shift(place[axis], d, 4)
+        fixed = {**fixed, axis: d - 1 if axis == "z" else target}
         at = {**place, axis: target}
         remote(
-            block(index, part), q[3 * part + step].at[(d - 1, *extra)],
+            block([fixed.get(a, slice(None)) for a in AXES], part),
+            q[3 * part + step].at[(d - 1, *extra)],
             q_send.at[part, step], q_recv.at[part, step],
             at["x"] * 8 + at["y"] * 2 + c, at["z"],
         ).start()
 
-    every = slice(None)
-    for n, dz in enumerate((2, 1, 3, 0)):
-        slab = shift(s, dz, NZ)
+    for n in range(NZ):
         merges[n].wait_recv()
 
         def merge(m, carry):
-            r_ref[slab, m // 4, lax.rem(m, 4)] += c_ref[slab, m // 4, lax.rem(m, 4), c]
+            r_ref[n, m // 4, lax.rem(m, 4)] += c_ref[n, m // 4, lax.rem(m, 4), c]
             return carry
 
-        lax.fori_loop(0, 16, merge, 0)
-        if dz:
-            hand_on(0, 0, dz, (slab, every, every), slab)
-        for d in (1, 3, 2):
-            target = shift(x, d, 4)
-            hand_on(1, 0, d, (slab, target, every), target, (slab,))
-            target = shift(y, d, 4)
-            hand_on(2, 0, d, (slab, every, target), target, (slab,))
+        lax.fori_loop(0, 16, merge, 0, unroll=4)
+        for d in (2, 1, 3):
+            if d == n + 1:
+                hand_on(0, 0, d, {})
+            hand_on(1, 0, d, {"z": n}, (n,))
+            hand_on(2, 0, d, {"z": n}, (n,))
 
     for step in range(3):
         for part, (row, rows, lane, lanes, order) in enumerate(PARTS):
             buffer = q[3 * part + step]
             settle(buffer, q_recv.at[part, step])
-            fixed = {a: place[a] for a in order[:step + 1]}
+            fixed = {a: own_at[a] for a in order[:step + 1]}
             free = [a for a in AXES if a not in fixed]
 
             def add(t, carry):
@@ -307,15 +314,12 @@
                 return carry
 
             if free:
-                lax.fori_loop(0, 4 ** len(free), add, 0)
+                lax.fori_loop(0, 4 ** len(free), add, 0, unroll=4)
             else:
                 add(0, 0)
             if step < 2:
-                axis = order[step + 1]
-                for d in (1, 3, 2):
-                    target = shift(place[axis], d, 4)
-                    at = {**fixed, axis: target}
-                    hand_on(part, step + 1, d, tuple(at.get(a, every) for a in AXES), target)
+                for d in (2, 1, 3):
+                    hand_on(part, step + 1, d, fixed)
 
     fin[...] = fin[...] / den[...]
     for i in range(VS // NZ):
@@ -341,6 +345,7 @@
         pltpu.VMEM((1024, widest), BF16),
         pltpu.VMEM((widest, 1024), BF16),
         pltpu.VMEM((widest, 1024), BF16),
+        pltpu.VMEM((1024, 1024), BF16),
         pltpu.VMEM((1024, 1024), BF16),
         pltpu.VMEM((8, 512), F32),
         pltpu.VMEM((LANES, 128), I32),
@@ -367,7 +372,7 @@
         out_specs=pl.BlockSpec(memory_space=pltpu.VMEM),
         scratch_shapes=scratch,
         compiler_params=pltpu.CompilerParams(
-            collective_id=0, has_side_effects=True, vmem_limit_bytes=52 << 20
+            collective_id=0, has_side_effects=True, vmem_limit_bytes=64 << 20
         ),
     )(amps, ints, irrep, occ, virt)
 

time: 71.7 us -> 67.1 us (0.936)
  Pallas kernels: 68.7 us -> 65.4 us
  local copies, waits for them, and re-layouts: 2.65 us -> 1.57 us
    pallas_call x1, Pallas kernels: 68.7 us -> 65.4 us  [contract(): pl.pallas_call(kernel, out_shape=jax.ShapeDtypeStruct((OCC * VS // NZ, VS...]
    unnamed x7 -> x1, local copies, waits for them, and re-layouts: 2.65 us -> 1.57 us
where the time goes in v3:
time: 67.1 us; the launch traced here: 67 us
  Pallas kernels  65.4 us (97%)
  local copies, waits for them, and re-layouts  1.57 us (2%)
    pallas_call x1, Pallas kernels, contract(): pl.pallas_call(kernel, out_shape=jax.ShapeDtypeStruct((OCC * VS // NZ, VS...  65.4 us
    unnamed x1, local copies, waits for them, and re-layouts  1.57 us

profile of v3, /device:TPU:0, one launch (start us, length us, event | category | flops | bytes accessed | tf_op | source)
XLA Modules:
  0.0 67.0 jit_solution(13143166713316899262)
XLA Ops:
  0.0 65.4 %shard_map.55 = f32[256,32]{1,0:T(8,128)} custom-call(bf16[32,160000]{1,0:T(8,128)(2,1)} %bitcast.6, bf16[625,8,256]{2,1,0:T(8,128)(2,1)} %bitcast.7, s32[1,400]{1,0:T(1,128)} %bitcast.9, f32[1,32]{1,0:T(1,128)} %bitcast.10, f32[1,32]{1,0:T(1,128)} %bitcast.11), custom_call_target="tpu_custom_call" | custom-call | tf_op jit(solution)/shard_map/pallas_call | solution.py:368
  65.4 1.6 %copy.7 = f32[1,32,8,32]{3,2,1,0:T(8,128)} copy(f32[1,32,8,32]{3,2,1,0:T(8,128)} %bitcast.8) | data formatting | bytes 65536

commit v4 on v3

v4 whole, which is shorter than its diff:
```python
import jax
import jax.numpy as jnp
from jax import lax
from jax.experimental import pallas as pl
from jax.experimental.pallas import tpu as pltpu
from jax.sharding import PartitionSpec as P

F32, BF16, I32 = jnp.float32, jnp.bfloat16, jnp.int32
V, VS, OCC = 400, 32, 32
NZ = 4
ROWS = 5000
GROUPS = ROWS // 8
LANES = 1280
SIZE = 256
NK = LANES // SIZE
MARGIN = 16
PARTS = (
    (0, 24, 0, 128, ("z", "x", "y")),
    (0, 24, 128, 128, ("x", "y", "z")),
    (24, 8, 0, 256, ("y", "z", "x")),
)
STEP_DIMS = ((4, 4), (4,), ())
AXES = ("z", "x", "y")


def shift(i, d, n):
    return lax.rem(i + d, n)


def remote(src, dst, send, recv, pair, slab):
    return pltpu.make_async_remote_copy(
        src_ref=src, dst_ref=dst, send_sem=send, recv_sem=recv,
        device_id={"pair": pair, "slab": slab}, device_id_type=pl.DeviceIdType.MESH,
    )


def settle(ref, sem):
    pltpu.make_async_copy(ref, ref, sem).wait()


def one_hot(test):
    return jnp.where(test, F32(1), F32(0)).astype(BF16)


def kernel(amps, ints, irrep, occ, virt, out, *refs):
    abuf, sib, bbuf, bm, bp = refs[:5]
    refs = refs[5:]
    ap, perm_own, perm_sib, perm_ab, vrow, rowirr, colirr, den, fin, c_ref = refs[:10]
    irrep_v, occ_s, virt_s = refs[10:13]
    q, via = refs[13:22], refs[22:25]
    a_send, b_send, x_send, a_recv, b_recv, x_recv, own_sem, arg_sem, v_send, v_recv, q_send, q_recv = (
        refs[25:]
    )

    p = lax.axis_index("pair")
    s = lax.axis_index("slab")
    x, y, c = p // 8, lax.rem(p // 2, 4), lax.rem(p, 2)
    place = {"z": s, "x": x, "y": y}
    chip = p // 2
    sibling = p + 1 - 2 * c

    def chip_at(dx, dy):
        return shift(x, dx, 4) * 4 + shift(y, dy, 4)

    barrier = pltpu.get_barrier_semaphore()

    def greet(pair, slab):
        pl.semaphore_signal(
            barrier, inc=1, device_id={"pair": pair, "slab": slab},
            device_id_type=pl.DeviceIdType.MESH,
        )

    def greet_some(dy, carry):
        for dx in (2, 1, 3, 0):
            greet(chip_at(dx, dy + dx) * 2 + c, s)
        return carry

    for dx in (2, 1, 3):
        greet(chip_at(dx, dx) * 2 + c, s)
    lax.fori_loop(1, 4, greet_some, 0)
    for dz in (2, 1, 3):
        greet(p, shift(s, dz, NZ))
    greet(sibling, s)
    small = [
        pltpu.make_async_copy(src, dst, arg_sem.at[i])
        for i, (src, dst) in enumerate(((irrep, irrep_v), (occ, occ_s), (virt, virt_s)))
    ]
    for copy in small:
        copy.start()
    pl.semaphore_wait(barrier, 19)

    first_tile = ROWS * p // 128
    lead = lax.rem(p, 16)

    def columns(pair, k):
        tile = ROWS * pair // 128 + 10 * s
        return pl.ds(pl.multiple_of(tile * 128 + k * SIZE, 128), SIZE)

    def rows_for(slab, k):
        want = 160 * slab - lead + k * (SIZE // 8)
        have = jnp.clip(want, 0, GROUPS - SIZE // 8)
        return pl.ds(have, SIZE // 8), pl.ds(MARGIN + have - want, SIZE // 8)

    def own_copies(k):
        source, target = rows_for(s, k)
        return [
            pltpu.make_async_copy(ints.at[source], bbuf.at[k, 3, target], own_sem.at[k, 2]),
        ] + [
            pltpu.make_async_copy(
                amps.at[:, columns(chip * 2 + w, k)], abuf.at[k, w, chip], own_sem.at[k, w]
            )
            for w in range(2)
        ]

    def send_amps(k, dx, dy, w):
        peer = chip_at(dx, dy) * 2
        remote(
            amps.at[:, columns(peer + w, k)], abuf.at[k, w, chip], a_send, a_recv.at[k], peer + c, s
        ).start()

    def send_chunk(k, carry):
        for dz in (1, 3, 2):
            slab = shift(s, dz, NZ)
            source, target = rows_for(slab, k)
            remote(
                ints.at[source], bbuf.at[k, 3 - dz, target], b_send, b_recv.at[k], p, slab
            ).start()
        for w in range(2):
            for dx in (1, 3, 2):
                send_amps(k, dx, dx, w)

        def send_some(i, carry):
            for dx in (1, 3, 2, 0):
                send_amps(k, dx, i // 2 + dx, lax.rem(i, 2))
            return carry

        lax.fori_loop(2, 8, send_some, 0)
        for copy in own_copies(k):
            copy.start()
        return carry

    lax.fori_loop(0, NK, send_chunk, 0)

    def orbitals(col):
        return ((((col >> 8) + s + 1) & 3) << 3) | ((col >> 5) & 7), col & 31

    def fill_perm(t, carry):
        row = lax.broadcasted_iota(I32, (128, 1024), 0) + t * 128
        col = lax.broadcasted_iota(I32, (128, 1024), 1)
        rows = pl.ds(pl.multiple_of(t * 128, 128), 128)
        a, b = orbitals(col)
        perm_ab[rows, :] = one_hot(
            row == (((((b >> 3) + 3 - s) & 3) << 8) | ((b & 7) << 5) | a)
        )
        return carry

    lax.fori_loop(0, 8, fill_perm, 0)

    def fill_swap(t, carry):
        row = lax.broadcasted_iota(I32, (128, 512), 0) + t * 128
        col = lax.broadcasted_iota(I32, (128, 512), 1)
        rows = pl.ds(pl.multiple_of(t * 128, 128), 128)
        i, j = ((row >> 5) << 1) + c, row & 31
        here = (((j >> 1) << 5) | i) == col
        perm_own[rows, :] = one_hot(here & ((j & 1) == c))
        perm_sib[rows, :] = one_hot(here & ((j & 1) != c))
        return carry

    lax.fori_loop(0, 4, fill_swap, 0)
    for copy in small:
        copy.wait()

    vrow[...] = jnp.zeros_like(vrow)
    vrow[0:1, 0:V] = irrep_v[...].astype(F32)
    table = jnp.broadcast_to(vrow[0:1, :], (128, 512)).astype(BF16)

    def look_up(lhs, rhs, dims):
        return lax.dot_general(
            lhs, rhs, (dims, ((), ())), preferred_element_type=F32
        ).astype(I32)

    orb = lax.broadcasted_iota(I32, (128, 1024), 0)
    col = lax.broadcasted_iota(I32, (128, 1024), 1)
    first = table[0:16, 0:128]
    of_a, of_b = (look_up(first, one_hot(orb == v), ((1,), (0,))) for v in orbitals(col))
    colirr[...] = (of_a ^ of_b)[0:8]

    start = (first_tile + 10 * s) * 128

    def fill_rows(t, carry):
        base = start + t * 256
        c0 = base // V
        row = lax.broadcasted_iota(I32, (256, 512), 0) + base
        orb = lax.broadcasted_iota(I32, (256, 512), 1)
        cc = jnp.where(row >= (c0 + 1) * V, c0 + 1, c0)
        of_c = look_up(one_hot(orb == cc), table, ((1,), (1,)))
        of_d = look_up(one_hot(orb == row - cc * V), table, ((1,), (1,)))
        row = row[:, 0:128]
        inside = (row >= ROWS * p) & (row < ROWS * p + ROWS)
        rowirr[pl.ds(pl.multiple_of(t * 256, 256), 256), :] = jnp.where(inside, of_c ^ of_d, -1)
        return carry

    lax.fori_loop(0, LANES // 256, fill_rows, 0)

    lane = lax.broadcasted_iota(I32, (8, 256), 1)
    row = lax.broadcasted_iota(I32, (32, 256), 0)
    of_a = jnp.zeros((8, 256), F32)
    of_b = jnp.zeros((8, 256), F32)
    of_j = jnp.zeros((32, 256), F32)
    for i in range(VS // NZ):
        of_a = jnp.where((lane >> 5) == i, virt_s[0, s * (VS // NZ) + i], of_a)
    for i in range(VS):
        of_b = jnp.where((lane & 31) == i, virt_s[0, i], of_b)
    for i in range(OCC):
        of_j = jnp.where(row == i, occ_s[0, i], of_j)
    den[...] = ((of_a + of_b) - occ_s[0, p])[0:1] - of_j

    own_at = {"z": 3, "x": x, "y": y}

    def block(index, part):
        row, rows, lane, lanes, _ = PARTS[part]
        return c_ref.at[(*index, pl.ds(row, rows), pl.ds(lane, lanes))]

    def peer_at(axis, d):
        at = {**place, axis: shift(place[axis], d, 4)}
        return at["x"] * 8 + at["y"] * 2 + c, at["z"]

    def share(axis, d):
        return d - 1 if axis == "z" else shift(place[axis], d, 4)

    def half(part, d, h):
        axis = PARTS[part][4][0]
        index = [share(axis, d) if a == axis else slice(None) for a in AXES]
        index[1 if axis == "z" else 0] = pl.ds(2 * h, 2)
        return block(index, part)

    def halfway(part, h):
        remote(
            half(part, 2, h), via[part].at[h], v_send.at[part], v_recv.at[part, h],
            *peer_at(PARTS[part][4][0], 3 if h else 1),
        ).start()

    def pass_on(part, d, h):
        remote(
            half(part, d, h), q[3 * part].at[0 if d == 1 else 1, pl.ds(2 * h, 2)],
            q_send.at[part, 0], q_recv.at[part, 0], *peer_at(PARTS[part][4][0], d),
        ).start()

    def begin(part):
        halfway(part, 0)
        halfway(part, 1)

    def straight(part):
        pass_on(part, 1, 1)
        pass_on(part, 3, 0)

    def hand_on(part, step, d, fixed):
        axis = PARTS[part][4][step]
        fixed = {**fixed, axis: share(axis, d)}
        remote(
            block([fixed.get(a, slice(None)) for a in AXES], part), q[3 * part + step].at[d - 1],
            q_send.at[part, step], q_recv.at[part, step], *peer_at(axis, d),
        ).start()

    def swap(src, dst, k, kind):
        return remote(src, dst, x_send.at[k, kind], x_recv.at[k, kind], sibling, s)

    def swap_ints(k):
        return swap(bm.at[k, c], bm.at[k, c], k, 0)

    def swap_amps(k):
        return swap(abuf.at[k], sib.at[k], k, 1)

    def clear(n, carry):
        c_ref[n] = jnp.zeros((4, 4, 32, 256), F32)
        return carry

    lax.fori_loop(0, NZ, clear, 0)

    def contract_chunk(k, carry):
        settle(abuf.at[k, :, pl.ds(0, 15)], a_recv.at[k])
        for copy in own_copies(k):
            copy.wait()
        swap_amps(k).start()
        settle(bbuf.at[k, pl.ds(0, 3), pl.ds(0, SIZE // 8)], b_recv.at[k])

        def mask(t, carry):
            rows = pl.multiple_of(t * 128, 128)
            row_irrep = rowirr[pl.ds(pl.multiple_of(k * SIZE + rows, 128), 128), :]
            for block in range(8):
                n, side = block // 2, block % 2
                part = bbuf[k, n, pl.ds(MARGIN + t * 16, 16), :, pl.ds(side * 128, 128)]
                part = part.astype(F32).reshape(128, 128)
                keep = row_irrep == colirr[0:1, block * 128:block * 128 + 128]
                bm[k, c, pl.ds(rows, 128), block * 128:block * 128 + 128] = jnp.where(
                    keep, part, F32(0)
                ).astype(BF16)
            return carry

        lax.fori_loop(0, SIZE // 128, mask, 0)
        swap_ints(k).start()

        def transpose(w):
            bp[w] = jnp.dot(bm[k, w], perm_ab[...], preferred_element_type=F32).astype(BF16)

        transpose(c)
        swap_amps(k).wait_recv()

        for w in range(2):
            mirrored = jnp.dot(
                perm_own[...], abuf[k, w].reshape(512, SIZE), preferred_element_type=F32
            ) + jnp.dot(perm_sib[...], sib[k, w].reshape(512, SIZE), preferred_element_type=F32)
            ap[w] = mirrored.astype(BF16)
        swap_ints(k).wait_recv()
        transpose(1 - c)
        for n in (1, 0, 2, 3):
            cols = slice(n * 256, n * 256 + 256)
            total = None
            for w in range(2):
                for left, right in (
                    (abuf[k, w].reshape(512, SIZE), bm[k, w, :, cols]), (ap[w], bp[w, :, cols])
                ):
                    term = jnp.dot(left, right, preferred_element_type=F32)
                    total = term if total is None else total + term
            c_ref[n] += total.reshape(4, 4, 32, 256)

            @pl.when(k == NK - 1)
            def _():
                if n == 1:
                    begin(0)
                elif n == 0:
                    halfway(1, 0)
                    halfway(2, 0)
                elif n == 2:
                    straight(0)
                else:
                    halfway(1, 1)
                    halfway(2, 1)
                    straight(1)
                    straight(2)

        return carry

    lax.fori_loop(0, NK, contract_chunk, 0)
    for part in range(3):
        for h, d in ((0, 1), (1, 3)):
            settle(via[part].at[h], v_recv.at[part, h])
            mine = half(part, d, h)

            def join(t, carry):
                i, j = t // 4, lax.rem(t, 4)
                mine[i, j] = mine[i, j] + via[part][h, i, j]
                return carry

            lax.fori_loop(0, 8, join, 0, unroll=2)
            pass_on(part, d, h)

    for step in range(3):
        for part, (row, rows, lane, lanes, order) in enumerate(PARTS):
            buffer = q[3 * part + step]
            settle(buffer, q_recv.at[part, step])
            fixed = {a: own_at[a] for a in order[:step + 1]}
            mine = block([fixed.get(a, slice(None)) for a in AXES], part)
            if step == 0:
                def add(t, carry):
                    i, j = t // 4, lax.rem(t, 4)
                    mine[i, j] = mine[i, j] + buffer[0, i, j] + buffer[1, i, j]
                    return carry

                lax.fori_loop(0, 16, add, 0, unroll=2)
            else:
                total = ((mine[...] + buffer[0]) + buffer[1]) + buffer[2]
                if step == 2:
                    fin[pl.ds(row, rows), pl.ds(lane, lanes)] = total
                    continue
                mine[...] = total
            for d in (2, 1, 3):
                hand_on(part, step + 1, d, fixed)

    fin[...] = fin[...] / den[...]
    for i in range(VS // NZ):
        out[pl.ds(i, 32, stride=VS // NZ), :] = fin[:, i * VS:i * VS + VS]

    def drain(k, carry):
        settle(abuf.at[k, :, pl.ds(0, 15)], a_send)
        settle(bbuf.at[k, pl.ds(0, 3), pl.ds(0, SIZE // 8)], b_send)
        swap_ints(k).wait_send()
        swap_amps(k).wait_send()
        return carry

    lax.fori_loop(0, NK, drain, 0)
    for part in range(3):
        for step in range(3):
            settle(q[3 * part + step], q_send.at[part, step])
        settle(via[part], v_send.at[part])


def contract(amps, ints, irrep, occ, virt):
    dma = pltpu.SemaphoreType.DMA
    scratch = [
        pltpu.VMEM((NK, 2, 16, 32, SIZE), BF16),
        pltpu.VMEM((NK, 2, 16, 32, SIZE), BF16),
        pltpu.VMEM((NK, NZ, SIZE // 8 + 2 * MARGIN, 8, 256), BF16),
        pltpu.VMEM((NK, 2, SIZE, 1024), BF16),
        pltpu.VMEM((2, SIZE, 1024), BF16),
        pltpu.VMEM((2, 512, SIZE), BF16),
        pltpu.VMEM((512, 512), BF16),
        pltpu.VMEM((512, 512), BF16),
        pltpu.VMEM((1024, 1024), BF16),
        pltpu.VMEM((8, 512), F32),
        pltpu.VMEM((LANES, 128), I32),
        pltpu.VMEM((8, 1024), I32),
        pltpu.VMEM((32, 256), F32),
        pltpu.VMEM((32, 256), F32),
        pltpu.VMEM((NZ, 4, 4, 32, 256), F32),
        pltpu.VMEM((1, V), I32),
        pltpu.SMEM((1, OCC), F32),
        pltpu.SMEM((1, VS), F32),
    ]
    for _, rows, _, lanes, _ in PARTS:
        for step, dims in enumerate(STEP_DIMS):
            scratch.append(pltpu.VMEM((3 if step else 2, *dims, rows, lanes), F32))
    scratch += [pltpu.VMEM((2, 2, 4, rows, lanes), F32) for _, rows, _, lanes, _ in PARTS]
    scratch += [
        dma, dma, dma((NK, 2)), dma((NK,)), dma((NK,)), dma((NK, 2)), dma((NK, 3)), dma((3,)),
        dma((3,)), dma((3, 2)), dma((3, 3)), dma((3, 3)),
    ]
    return pl.pallas_call(
        kernel,
        out_shape=jax.ShapeDtypeStruct((OCC * VS // NZ, VS), F32),
        in_specs=[pl.BlockSpec(memory_space=pltpu.HBM)] * 5,
        out_specs=pl.BlockSpec(memory_space=pltpu.VMEM),
        scratch_shapes=scratch,
        compiler_params=pltpu.CompilerParams(
            collective_id=0, has_side_effects=True, vmem_limit_bytes=64 << 20
        ),
    )(amps, ints, irrep, occ, virt)


def local(amplitudes, integrals, virt_irrep, occ_energy, slab_energy):
    update = contract(
        amplitudes.reshape(OCC, V * V), integrals.reshape(GROUPS, 8, 256),
        virt_irrep.reshape(1, V), occ_energy.reshape(1, OCC), slab_energy.reshape(1, VS),
    )
    return update.reshape(1, OCC, VS // NZ, VS)


def solution(mesh):
    placed = (P("pair", None, None), P("pair", "slab"), P(), P(), P())
    return jax.shard_map(
        local, mesh=mesh, in_specs=placed, out_specs=P("pair", None, "slab", None), check_vma=False
    )
```

time: 67.1 us -> 68.9 us (1.027)
  Pallas kernels: 65.4 us -> 67.2 us
    pallas_call x1, Pallas kernels: 65.4 us -> 67.2 us  [contract(): pl.pallas_call(kernel, out_shape=jax.ShapeDtypeStruct((OCC * VS // NZ, VS...]
where the time goes in v4:
time: 68.9 us; the launch traced here: 68.8 us
  Pallas kernels  67.2 us (98%)
  local copies, waits for them, and re-layouts  1.57 us (2%)
    pallas_call x1, Pallas kernels, contract(): pl.pallas_call(kernel, out_shape=jax.ShapeDtypeStruct((OCC * VS // NZ, VS...  67.2 us
    unnamed x1, local copies, waits for them, and re-layouts  1.57 us

profile of v4, /device:TPU:0, one launch (start us, length us, event | category | flops | bytes accessed | tf_op | source)
XLA Modules:
  0.0 68.8 jit_solution(3887260782891238030)
XLA Ops:
  0.0 67.2 %shard_map.55 = f32[256,32]{1,0:T(8,128)} custom-call(bf16[32,160000]{1,0:T(8,128)(2,1)} %bitcast.6, bf16[625,8,256]{2,1,0:T(8,128)(2,1)} %bitcast.7, s32[1,400]{1,0:T(1,128)} %bitcast.9, f32[1,32]{1,0:T(1,128)} %bitcast.10, f32[1,32]{1,0:T(1,128)} %bitcast.11), custom_call_target="tpu_custom_call" | custom-call | tf_op jit(solution)/shard_map/pallas_call | solution.py:428
  67.2 1.6 %copy.7 = f32[1,32,8,32]{3,2,1,0:T(8,128)} copy(f32[1,32,8,32]{3,2,1,0:T(8,128)} %bitcast.8) | data formatting | bytes 65536

commit v5 on v4

--- a/solution.py
+++ b/solution.py
@@ -20,7 +20,6 @@
     (24, 8, 0, 256, ("y", "z", "x")),
 )
 STEP_DIMS = ((4, 4), (4,), ())
-AXES = ("z", "x", "y")
 
 
 def shift(i, d, n):
@@ -45,11 +44,12 @@
 def kernel(amps, ints, irrep, occ, virt, out, *refs):
     abuf, sib, bbuf, bm, bp = refs[:5]
     refs = refs[5:]
-    ap, perm_own, perm_sib, perm_ab, vrow, rowirr, colirr, den, fin, c_ref = refs[:10]
-    irrep_v, occ_s, virt_s = refs[10:13]
-    q, via = refs[13:22], refs[22:25]
+    ap, perm_own, perm_sib, perm_ab, vrow, rowirr, colirr, den, fin = refs[:9]
+    sums, refs = refs[9:12], refs[12:]
+    irrep_v, occ_s, virt_s = refs[:3]
+    q, via = refs[3:12], refs[12:15]
     a_send, b_send, x_send, a_recv, b_recv, x_recv, own_sem, arg_sem, v_send, v_recv, q_send, q_recv = (
-        refs[25:]
+        refs[15:]
     )
 
     p = lax.axis_index("pair")
@@ -217,10 +217,6 @@
 
     own_at = {"z": 3, "x": x, "y": y}
 
-    def block(index, part):
-        row, rows, lane, lanes, _ = PARTS[part]
-        return c_ref.at[(*index, pl.ds(row, rows), pl.ds(lane, lanes))]
-
     def peer_at(axis, d):
         at = {**place, axis: shift(place[axis], d, 4)}
         return at["x"] * 8 + at["y"] * 2 + c, at["z"]
@@ -229,10 +225,7 @@
         return d - 1 if axis == "z" else shift(place[axis], d, 4)
 
     def half(part, d, h):
-        axis = PARTS[part][4][0]
-        index = [share(axis, d) if a == axis else slice(None) for a in AXES]
-        index[1 if axis == "z" else 0] = pl.ds(2 * h, 2)
-        return block(index, part)
+        return sums[part].at[share(PARTS[part][4][0], d), pl.ds(2 * h, 2)]
 
     def halfway(part, h):
         remote(
@@ -254,12 +247,12 @@
         pass_on(part, 1, 1)
         pass_on(part, 3, 0)
 
-    def hand_on(part, step, d, fixed):
-        axis = PARTS[part][4][step]
-        fixed = {**fixed, axis: share(axis, d)}
+    def hand_on(part, step, d):
+        order = PARTS[part][4]
         remote(
-            block([fixed.get(a, slice(None)) for a in AXES], part), q[3 * part + step].at[d - 1],
-            q_send.at[part, step], q_recv.at[part, step], *peer_at(axis, d),
+            sums[part].at[(*[own_at[a] for a in order[:step]], share(order[step], d))],
+            q[3 * part + step].at[d - 1],
+            q_send.at[part, step], q_recv.at[part, step], *peer_at(order[step], d),
         ).start()
 
     def swap(src, dst, k, kind):
@@ -272,17 +265,15 @@
         return swap(abuf.at[k], sib.at[k], k, 1)
 
     def clear(n, carry):
-        c_ref[n] = jnp.zeros((4, 4, 32, 256), F32)
-        return carry
-
-    lax.fori_loop(0, NZ, clear, 0)
+        for part in sums:
+            part[n] = jnp.zeros(part.shape[1:], F32)
+        return carry
+
+    lax.fori_loop(0, 4, clear, 0)
 
     def contract_chunk(k, carry):
-        settle(abuf.at[k, :, pl.ds(0, 15)], a_recv.at[k])
-        for copy in own_copies(k):
-            copy.wait()
-        swap_amps(k).start()
         settle(bbuf.at[k, pl.ds(0, 3), pl.ds(0, SIZE // 8)], b_recv.at[k])
+        own_copies(k)[0].wait()
 
         def mask(t, carry):
             rows = pl.multiple_of(t * 128, 128)
@@ -304,6 +295,12 @@
             bp[w] = jnp.dot(bm[k, w], perm_ab[...], preferred_element_type=F32).astype(BF16)
 
         transpose(c)
+        settle(abuf.at[k, :, pl.ds(0, 15)], a_recv.at[k])
+        for copy in own_copies(k)[1:]:
+            copy.wait()
+        swap_amps(k).start()
+        swap_ints(k).wait_recv()
+        transpose(1 - c)
         swap_amps(k).wait_recv()
 
         for w in range(2):
@@ -311,9 +308,7 @@
                 perm_own[...], abuf[k, w].reshape(512, SIZE), preferred_element_type=F32
             ) + jnp.dot(perm_sib[...], sib[k, w].reshape(512, SIZE), preferred_element_type=F32)
             ap[w] = mirrored.astype(BF16)
-        swap_ints(k).wait_recv()
-        transpose(1 - c)
-        for n in (1, 0, 2, 3):
+        for n in range(NZ):
             cols = slice(n * 256, n * 256 + 256)
             total = None
             for w in range(2):
@@ -322,60 +317,45 @@
                 ):
                     term = jnp.dot(left, right, preferred_element_type=F32)
                     total = term if total is None else total + term
-            c_ref[n] += total.reshape(4, 4, 32, 256)
-
-            @pl.when(k == NK - 1)
-            def _():
-                if n == 1:
-                    begin(0)
-                elif n == 0:
-                    halfway(1, 0)
-                    halfway(2, 0)
-                elif n == 2:
-                    straight(0)
-                else:
-                    halfway(1, 1)
-                    halfway(2, 1)
-                    straight(1)
-                    straight(2)
-
+            total = total.reshape(4, 4, 32, 256)
+            for part, (row, rows, lane, lanes, order) in zip(sums, PARTS):
+                for i in range(4):
+                    for j in range(4):
+                        at = {"z": n, "x": i, "y": j}
+                        part[tuple(at[a] for a in order)] += total[
+                            i, j, row:row + rows, lane:lane + lanes
+                        ]
         return carry
 
     lax.fori_loop(0, NK, contract_chunk, 0)
+    begin(0)
+    for h in range(2):
+        halfway(1, h)
+        halfway(2, h)
+    for part in range(3):
+        straight(part)
     for part in range(3):
         for h, d in ((0, 1), (1, 3)):
             settle(via[part].at[h], v_recv.at[part, h])
             mine = half(part, d, h)
 
-            def join(t, carry):
-                i, j = t // 4, lax.rem(t, 4)
-                mine[i, j] = mine[i, j] + via[part][h, i, j]
-                return carry
-
-            lax.fori_loop(0, 8, join, 0, unroll=2)
+            mine[...] = mine[...] + via[part][h]
             pass_on(part, d, h)
 
     for step in range(3):
         for part, (row, rows, lane, lanes, order) in enumerate(PARTS):
             buffer = q[3 * part + step]
             settle(buffer, q_recv.at[part, step])
-            fixed = {a: own_at[a] for a in order[:step + 1]}
-            mine = block([fixed.get(a, slice(None)) for a in AXES], part)
-            if step == 0:
-                def add(t, carry):
-                    i, j = t // 4, lax.rem(t, 4)
-                    mine[i, j] = mine[i, j] + buffer[0, i, j] + buffer[1, i, j]
-                    return carry
-
-                lax.fori_loop(0, 16, add, 0, unroll=2)
-            else:
-                total = ((mine[...] + buffer[0]) + buffer[1]) + buffer[2]
-                if step == 2:
-                    fin[pl.ds(row, rows), pl.ds(lane, lanes)] = total
-                    continue
-                mine[...] = total
+            mine = sums[part].at[tuple(own_at[a] for a in order[:step + 1])]
+            total = mine[...]
+            for d in range(3 if step else 2):
+                total = total + buffer[d]
+            if step == 2:
+                fin[pl.ds(row, rows), pl.ds(lane, lanes)] = total
+                continue
+            mine[...] = total
             for d in (2, 1, 3):
-                hand_on(part, step + 1, d, fixed)
+                hand_on(part, step + 1, d)
 
     fin[...] = fin[...] / den[...]
     for i in range(VS // NZ):
@@ -412,7 +392,7 @@
         pltpu.VMEM((8, 1024), I32),
         pltpu.VMEM((32, 256), F32),
         pltpu.VMEM((32, 256), F32),
-        pltpu.VMEM((NZ, 4, 4, 32, 256), F32),
+        *[pltpu.VMEM((4, 4, 4, rows, lanes), F32) for _, rows, _, lanes, _ in PARTS],
         pltpu.VMEM((1, V), I32),
         pltpu.SMEM((1, OCC), F32),
         pltpu.SMEM((1, VS), F32),

time: 68.9 us -> 64.5 us (0.936)
  Pallas kernels: 67.2 us -> 62.8 us
    pallas_call x1, Pallas kernels: 67.2 us -> 62.8 us  [contract(): pl.pallas_call(kernel, out_shape=jax.ShapeDtypeStruct((OCC * VS // NZ, VS...]
where the time goes in v5:
time: 64.5 us; the launch traced here: 64.4 us
  Pallas kernels  62.8 us (97%)
  local copies, waits for them, and re-layouts  1.57 us (2%)
    pallas_call x1, Pallas kernels, contract(): pl.pallas_call(kernel, out_shape=jax.ShapeDtypeStruct((OCC * VS // NZ, VS...  62.8 us
    unnamed x1, local copies, waits for them, and re-layouts  1.57 us

profile of v5, /device:TPU:0, one launch (start us, length us, event | category | flops | bytes accessed | tf_op | source)
XLA Modules:
  0.0 64.4 jit_solution(9856568627213629015)
XLA Ops:
  0.0 62.8 %shard_map.55 = f32[256,32]{1,0:T(8,128)} custom-call(bf16[32,160000]{1,0:T(8,128)(2,1)} %bitcast.6, bf16[625,8,256]{2,1,0:T(8,128)(2,1)} %bitcast.7, s32[1,400]{1,0:T(1,128)} %bitcast.9, f32[1,32]{1,0:T(1,128)} %bitcast.10, f32[1,32]{1,0:T(1,128)} %bitcast.11), custom_call_target="tpu_custom_call" | custom-call | tf_op jit(solution)/shard_map/pallas_call | solution.py:408
  62.8 1.6 %copy.7 = f32[1,32,8,32]{3,2,1,0:T(8,128)} copy(f32[1,32,8,32]{3,2,1,0:T(8,128)} %bitcast.8) | data formatting | bytes 65536

commit v6 on v5

--- a/solution.py
+++ b/solution.py
@@ -15,10 +15,13 @@
 NK = LANES // SIZE
 MARGIN = 16
 PARTS = (
-    (0, 24, 0, 128, ("z", "x", "y")),
-    (0, 24, 128, 128, ("x", "y", "z")),
+    (0, 16, 0, 128, ("z", "x", "y")),
+    (0, 16, 128, 128, ("x", "y", "z")),
     (24, 8, 0, 256, ("y", "z", "x")),
+    (16, 8, 0, 128, ("z", "x", "y")),
+    (16, 8, 128, 128, ("x", "y", "z")),
 )
+NP = len(PARTS)
 STEP_DIMS = ((4, 4), (4,), ())
 
 
@@ -45,11 +48,11 @@
     abuf, sib, bbuf, bm, bp = refs[:5]
     refs = refs[5:]
     ap, perm_own, perm_sib, perm_ab, vrow, rowirr, colirr, den, fin = refs[:9]
-    sums, refs = refs[9:12], refs[12:]
+    sums, refs = refs[9:9 + NP], refs[9 + NP:]
     irrep_v, occ_s, virt_s = refs[:3]
-    q, via = refs[3:12], refs[12:15]
+    q, via = refs[3:3 + 3 * NP], refs[3 + 3 * NP:3 + 4 * NP]
     a_send, b_send, x_send, a_recv, b_recv, x_recv, own_sem, arg_sem, v_send, v_recv, q_send, q_recv = (
-        refs[15:]
+        refs[3 + 4 * NP:]
     )
 
     p = lax.axis_index("pair")
@@ -328,13 +331,19 @@
         return carry
 
     lax.fori_loop(0, NK, contract_chunk, 0)
-    begin(0)
-    for h in range(2):
-        halfway(1, h)
-        halfway(2, h)
-    for part in range(3):
+    for part in range(NP):
+        begin(part)
         straight(part)
-    for part in range(3):
+
+    def drain(k, carry):
+        settle(abuf.at[k, :, pl.ds(0, 15)], a_send)
+        settle(bbuf.at[k, pl.ds(0, 3), pl.ds(0, SIZE // 8)], b_send)
+        swap_ints(k).wait_send()
+        swap_amps(k).wait_send()
+        return carry
+
+    lax.fori_loop(0, NK, drain, 0)
+    for part in range(NP):
         for h, d in ((0, 1), (1, 3)):
             settle(via[part].at[h], v_recv.at[part, h])
             mine = half(part, d, h)
@@ -361,15 +370,7 @@
     for i in range(VS // NZ):
         out[pl.ds(i, 32, stride=VS // NZ), :] = fin[:, i * VS:i * VS + VS]
 
-    def drain(k, carry):
-        settle(abuf.at[k, :, pl.ds(0, 15)], a_send)
-        settle(bbuf.at[k, pl.ds(0, 3), pl.ds(0, SIZE // 8)], b_send)
-        swap_ints(k).wait_send()
-        swap_amps(k).wait_send()
-        return carry
-
-    lax.fori_loop(0, NK, drain, 0)
-    for part in range(3):
+    for part in range(NP):
         for step in range(3):
             settle(q[3 * part + step], q_send.at[part, step])
         settle(via[part], v_send.at[part])
@@ -403,7 +404,7 @@
     scratch += [pltpu.VMEM((2, 2, 4, rows, lanes), F32) for _, rows, _, lanes, _ in PARTS]
     scratch += [
         dma, dma, dma((NK, 2)), dma((NK,)), dma((NK,)), dma((NK, 2)), dma((NK, 3)), dma((3,)),
-        dma((3,)), dma((3, 2)), dma((3, 3)), dma((3, 3)),
+        dma((NP,)), dma((NP, 2)), dma((NP, 3)), dma((NP, 3)),
     ]
     return pl.pallas_call(
         kernel,

time: 64.5 us -> 63.8 us (0.989)
  Pallas kernels: 62.8 us -> 61.9 us
    pallas_call x1, Pallas kernels: 62.8 us -> 61.9 us  [contract(): pl.pallas_call(kernel, out_shape=jax.ShapeDtypeStruct((OCC * VS // NZ, VS...]
where the time goes in v6:
time: 63.8 us; the launch traced here: 63.5 us
  Pallas kernels  61.9 us (97%)
  local copies, waits for them, and re-layouts  1.57 us (2%)
    pallas_call x1, Pallas kernels, contract(): pl.pallas_call(kernel, out_shape=jax.ShapeDtypeStruct((OCC * VS // NZ, VS...  61.9 us
    unnamed x1, local copies, waits for them, and re-layouts  1.57 us

profile of v6, /device:TPU:0, one launch (start us, length us, event | category | flops | bytes accessed | tf_op | source)
XLA Modules:
  0.0 63.5 jit_solution(6881856175772398444)
XLA Ops:
  0.0 61.9 %shard_map.55 = f32[256,32]{1,0:T(8,128)} custom-call(bf16[32,160000]{1,0:T(8,128)(2,1)} %bitcast.6, bf16[625,8,256]{2,1,0:T(8,128)(2,1)} %bitcast.7, s32[1,400]{1,0:T(1,128)} %bitcast.9, f32[1,32]{1,0:T(1,128)} %bitcast.10, f32[1,32]{1,0:T(1,128)} %bitcast.11), custom_call_target="tpu_custom_call" | custom-call | tf_op jit(solution)/shard_map/pallas_call | solution.py:409
  62.0 1.6 %copy.7 = f32[1,32,8,32]{3,2,1,0:T(8,128)} copy(f32[1,32,8,32]{3,2,1,0:T(8,128)} %bitcast.8) | data formatting | bytes 65536

commit v7 on v6

--- a/solution.py
+++ b/solution.py
@@ -118,7 +118,7 @@
     def send_amps(k, dx, dy, w):
         peer = chip_at(dx, dy) * 2
         remote(
-            amps.at[:, columns(peer + w, k)], abuf.at[k, w, chip], a_send, a_recv.at[k], peer + c, s
+            amps.at[:, columns(peer + w, k)], abuf.at[k, w, chip], a_send, a_recv.at[k, w], peer + c, s
         ).start()
 
     def send_chunk(k, carry):
@@ -128,16 +128,18 @@
             remote(
                 ints.at[source], bbuf.at[k, 3 - dz, target], b_send, b_recv.at[k], p, slab
             ).start()
-        for w in range(2):
+        def send_range(w, carry):
             for dx in (1, 3, 2):
                 send_amps(k, dx, dx, w)
 
-        def send_some(i, carry):
-            for dx in (1, 3, 2, 0):
-                send_amps(k, dx, i // 2 + dx, lax.rem(i, 2))
-            return carry
-
-        lax.fori_loop(2, 8, send_some, 0)
+            def send_some(dy, carry):
+                for dx in (1, 3, 2, 0):
+                    send_amps(k, dx, dy + dx, w)
+                return carry
+
+            return lax.fori_loop(1, 4, send_some, carry)
+
+        lax.fori_loop(0, 2, send_range, 0)
         for copy in own_copies(k):
             copy.start()
         return carry
@@ -264,8 +266,8 @@
     def swap_ints(k):
         return swap(bm.at[k, c], bm.at[k, c], k, 0)
 
-    def swap_amps(k):
-        return swap(abuf.at[k], sib.at[k], k, 1)
+    def swap_amps(k, w):
+        return swap(abuf.at[k, w], sib.at[k, w], k, 1 + w)
 
     def clear(n, carry):
         for part in sums:
@@ -291,20 +293,22 @@
                 ).astype(BF16)
             return carry
 
-        lax.fori_loop(0, SIZE // 128, mask, 0)
+        lax.fori_loop(0, SIZE // 128, mask, 0, unroll=True)
         swap_ints(k).start()
 
         def transpose(w):
             bp[w] = jnp.dot(bm[k, w], perm_ab[...], preferred_element_type=F32).astype(BF16)
 
         transpose(c)
-        settle(abuf.at[k, :, pl.ds(0, 15)], a_recv.at[k])
-        for copy in own_copies(k)[1:]:
-            copy.wait()
-        swap_amps(k).start()
+        own = own_copies(k)[1:]
+        for w in range(2):
+            settle(abuf.at[k, w, pl.ds(0, 15)], a_recv.at[k, w])
+            own[w].wait()
+            swap_amps(k, w).start()
         swap_ints(k).wait_recv()
         transpose(1 - c)
-        swap_amps(k).wait_recv()
+        swap_amps(k, 0).wait_recv()
+        swap_amps(k, 1).wait_recv()
 
         for w in range(2):
             mirrored = jnp.dot(
@@ -333,13 +337,15 @@
     lax.fori_loop(0, NK, contract_chunk, 0)
     for part in range(NP):
         begin(part)
+    for part in range(NP):
         straight(part)
 
     def drain(k, carry):
         settle(abuf.at[k, :, pl.ds(0, 15)], a_send)
         settle(bbuf.at[k, pl.ds(0, 3), pl.ds(0, SIZE // 8)], b_send)
         swap_ints(k).wait_send()
-        swap_amps(k).wait_send()
+        swap_amps(k, 0).wait_send()
+        swap_amps(k, 1).wait_send()
         return carry
 
     lax.fori_loop(0, NK, drain, 0)
@@ -403,7 +409,7 @@
             scratch.append(pltpu.VMEM((3 if step else 2, *dims, rows, lanes), F32))
     scratch += [pltpu.VMEM((2, 2, 4, rows, lanes), F32) for _, rows, _, lanes, _ in PARTS]
     scratch += [
-        dma, dma, dma((NK, 2)), dma((NK,)), dma((NK,)), dma((NK, 2)), dma((NK, 3)), dma((3,)),
+        dma, dma, dma((NK, 3)), dma((NK, 2)), dma((NK,)), dma((NK, 3)), dma((NK, 3)), dma((3,)),
         dma((NP,)), dma((NP, 2)), dma((NP, 3)), dma((NP, 3)),
     ]
     return pl.pallas_call(

time: 63.8 us -> 62.3 us (0.976)
  Pallas kernels: 61.9 us -> 60.6 us
    pallas_call x1, Pallas kernels: 61.9 us -> 60.6 us  [contract(): pl.pallas_call(kernel, out_shape=jax.ShapeDtypeStruct((OCC * VS // NZ, VS...]
where the time goes in v7:
time: 62.3 us; the launch traced here: 62.2 us
  Pallas kernels  60.6 us (97%)
  local copies, waits for them, and re-layouts  1.57 us (3%)
    pallas_call x1, Pallas kernels, contract(): pl.pallas_call(kernel, out_shape=jax.ShapeDtypeStruct((OCC * VS // NZ, VS...  60.6 us
    unnamed x1, local copies, waits for them, and re-layouts  1.57 us

profile of v7, /device:TPU:0, one launch (start us, length us, event | category | flops | bytes accessed | tf_op | source)
XLA Modules:
  0.0 62.2 jit_solution(15178357563440728153)
XLA Ops:
  0.0 60.6 %shard_map.55 = f32[256,32]{1,0:T(8,128)} custom-call(bf16[32,160000]{1,0:T(8,128)(2,1)} %bitcast.6, bf16[625,8,256]{2,1,0:T(8,128)(2,1)} %bitcast.7, s32[1,400]{1,0:T(1,128)} %bitcast.9, f32[1,32]{1,0:T(1,128)} %bitcast.10, f32[1,32]{1,0:T(1,128)} %bitcast.11), custom_call_target="tpu_custom_call" | custom-call | tf_op jit(solution)/shard_map/pallas_call | solution.py:415
  60.6 1.6 %copy.7 = f32[1,32,8,32]{3,2,1,0:T(8,128)} copy(f32[1,32,8,32]{3,2,1,0:T(8,128)} %bitcast.8) | data formatting | bytes 65536

commit v8 on v7

--- a/solution.py
+++ b/solution.py
@@ -17,9 +17,10 @@
 PARTS = (
     (0, 16, 0, 128, ("z", "x", "y")),
     (0, 16, 128, 128, ("x", "y", "z")),
-    (24, 8, 0, 256, ("y", "z", "x")),
+    (24, 8, 0, 128, ("y", "z", "x")),
     (16, 8, 0, 128, ("z", "x", "y")),
     (16, 8, 128, 128, ("x", "y", "z")),
+    (24, 8, 128, 128, ("y", "z", "x")),
 )
 NP = len(PARTS)
 STEP_DIMS = ((4, 4), (4,), ())

time: 62.3 us -> 62.4 us (level)
  no operation moved by 1% of the time
where the time goes in v8:
time: 62.4 us; the launch traced here: 62.3 us
  Pallas kernels  60.7 us (97%)
  local copies, waits for them, and re-layouts  1.57 us (3%)
    pallas_call x1, Pallas kernels, contract(): pl.pallas_call(kernel, out_shape=jax.ShapeDtypeStruct((OCC * VS // NZ, VS...  60.7 us
    unnamed x1, local copies, waits for them, and re-layouts  1.57 us

profile of v8, /device:TPU:0, one launch (start us, length us, event | category | flops | bytes accessed | tf_op | source)
XLA Modules:
  0.0 62.3 jit_solution(15605741829761518742)
XLA Ops:
  0.0 60.7 %shard_map.55 = f32[256,32]{1,0:T(8,128)} custom-call(bf16[32,160000]{1,0:T(8,128)(2,1)} %bitcast.6, bf16[625,8,256]{2,1,0:T(8,128)(2,1)} %bitcast.7, s32[1,400]{1,0:T(1,128)} %bitcast.9, f32[1,32]{1,0:T(1,128)} %bitcast.10, f32[1,32]{1,0:T(1,128)} %bitcast.11), custom_call_target="tpu_custom_call" | custom-call | tf_op jit(solution)/shard_map/pallas_call | solution.py:416
  60.7 1.6 %copy.7 = f32[1,32,8,32]{3,2,1,0:T(8,128)} copy(f32[1,32,8,32]{3,2,1,0:T(8,128)} %bitcast.8) | data formatting | bytes 65536
